TPU v7x, 256 devices: a whole 4x4x8 slice. The times are simulated.
256 devices in a mesh: lon: 16 (over z, x_lo), lat: 16 (over x_hi, y, core).
Axes of the slice: x: 4 (x_hi: 2, x_lo: 2; x = x_hi * 2 + x_lo), y: 4, z: 8, core: 2. Of those that a mesh axis runs over, the one named last changes fastest.
Arguments:
- tracer: float32 [4, 12, 1024, 4096], P(None, None, 'lat', 'lon'), may hold values from -6 to 6
- east_velocity: float32 [12, 1024, 4096], P(None, 'lat', 'lon'), may hold values from -0.25 to 0.25
- north_velocity: float32 [12, 1024, 4096], P(None, 'lat', 'lon'), may hold values from -0.25 to 0.25
- diffusivity: float32 [12, 1024, 4096], P(None, 'lat', 'lon'), may hold values from 0.01 to 0.12
- east_slope: float32 [12, 1024, 4096], P(None, 'lat', 'lon'), may hold values from -0.5 to 0.5
- north_slope: float32 [12, 1024, 4096], P(None, 'lat', 'lon'), may hold values from -0.5 to 0.5
- vertical_diffusivity: float32 [11, 1024, 4096], P(None, 'lat', 'lon'), may hold values from 0.1 to 10
- sea_mask: int32 [12, 1024, 4096], P(None, 'lat', 'lon'), may hold values from 0 to 1, as said below
- bottom: int32 [1024, 4096], P('lat', 'lon'), may hold values from 0 to 12, as said below
Outputs:
- updated: float32 [4, 12, 1024, 4096], P(None, None, 'lat', 'lon')
Inputs may be any that keep to these rules, and one draw needn't show every extreme that they name: sea_mask is 1 exactly at the levels k < bottom of its column. `bottom`: 0 marks a land column.
All inputs are finite; a program needn't handle non-finite values.
Results may differ from a plain program's by a relative error of at most 0.0003.
Values sent between devices are 32-bit elements; how exact they have to be, the bound alone decides.
No kernel may reach another device: no remote copies, remote signals or barrier semaphores. Data moves between devices by JAX's collectives and lax.ppermute only.
A program may use at most 128 MiB of HBM per device.

v0:
```python
import jax
import jax.numpy as jnp
from jax import lax
from jax.experimental import pallas as pl
from jax.experimental.pallas import tpu as pltpu
from jax.sharding import PartitionSpec as P

F32 = jnp.float32
LANES = 128
ROWS = 8


def iota(shape, dim):
    return lax.broadcasted_iota(jnp.int32, shape, dim)


def minmod(first, second):
    return jnp.minimum(
        jnp.maximum(second, jnp.minimum(first, 0.0)), jnp.maximum(first, 0.0)
    )


def limiter_weight(speed):
    size = jnp.abs(speed)
    return 0.5 * size * (1.0 - size)


def pack_kernel(levels, tracers, rows, cols, lon_name, lat_name, *refs):
    (
        tracer_hbm,
        east_vel_hbm,
        north_vel_hbm,
        diff_hbm,
        east_slope_hbm,
        north_slope_hbm,
        bottom_hbm,
        pay_a,
        pay_b,
        pay_c,
        pay_d,
        own_lon,
        own_lat,
        own_lat_coef,
        tracer_v,
        east_vel_v,
        diff_v,
        east_slope_v,
        north_v,
        bottom_v,
        sems,
        row_sems,
    ) = refs
    items = levels * tracers
    group = 3
    groups = levels // group
    last = rows - ROWS
    copies = []
    row_copies = [pltpu.make_async_copy(bottom_hbm, bottom_v, row_sems.at[0])]
    for n, (src, start) in enumerate(
        ((north_vel_hbm, 0), (north_vel_hbm, last), (north_slope_hbm, 0), (north_slope_hbm, last))
    ):
        row_copies.append(
            pltpu.make_async_copy(
                src.at[:, pl.ds(start, ROWS), :], north_v.at[n], row_sems.at[n + 1]
            )
        )
    for g in range(groups):
        span = pl.ds(g * group, group)
        fetch = [
            pltpu.make_async_copy(
                tracer_hbm.at[:, span], tracer_v.at[:, span], sems.at[g, 0]
            )
        ]
        for n, (src, dst) in enumerate(
            ((diff_hbm, diff_v), (east_vel_hbm, east_vel_v), (east_slope_hbm, east_slope_v))
        ):
            fetch.append(pltpu.make_async_copy(src.at[span], dst.at[span], sems.at[g, n + 1]))
        copies.append(fetch)
    for copy in copies[0]:
        copy.start()
    for copy in row_copies:
        copy.start()
    for fetch in copies[1:]:
        for copy in fetch:
            copy.start()

    lane = iota((rows, LANES), 1)
    sub = iota((ROWS, cols), 0)
    right = cols - LANES
    zero = jnp.zeros((rows, LANES), F32)
    cells = [zero] * 6
    d_cols, v_cols, s_cols = [zero] * 4, [zero] * 3, [zero] * 3
    row_at = (0, 1, 2, rows - 3, rows - 2, rows - 1)
    for copy in row_copies:
        copy.wait()
    row_bottoms = [bottom_v[r : r + 1, :] for r in row_at]
    block = [[jnp.zeros((ROWS, cols), F32)] * 6 for _ in range(items // ROWS)]
    edge_bottom = jnp.where(lane < 64, bottom_v[:, :LANES], bottom_v[:, right:])

    def ends(ref, index):
        return jnp.where(lane < 64, ref[index][:, :LANES], ref[index][:, right:])

    for g in range(groups):
        for copy in copies[g]:
            copy.wait()
        for k in range(g * group, (g + 1) * group):
            sea = edge_bottom > k
            for t in range(tracers):
                n = k * tracers + t
                both = jnp.where(sea, jnp.where(
                    lane < 64, tracer_v[t, k, :, :LANES], tracer_v[t, k, :, right:]), 0.0)
                turned = pltpu.roll(both, n, axis=1) if n else both
                for c in range(6):
                    place = (n + (c if c < 3 else c - 6)) % LANES
                    cells[c] = jnp.where(lane == place, turned, cells[c])
                for c, r in enumerate(row_at):
                    row = jnp.where(row_bottoms[c] > k, tracer_v[t, k, r : r + 1, :], 0.0)
                    block[n // ROWS][c] = jnp.where(
                        sub == n % ROWS, jnp.broadcast_to(row, (ROWS, cols)), block[n // ROWS][c]
                    )
            n = k * tracers
            for ref, outs, places in (
                (diff_v, d_cols, (0, 1, -2, -1)),
                (east_vel_v, v_cols, (0, -2, -1)),
                (east_slope_v, s_cols, (0, -2, -1)),
            ):
                both = jnp.where(lane < 64, ref[k, :, :LANES], ref[k, :, right:])
                turned = pltpu.roll(both, n, axis=1) if n else both
                for c, off in enumerate(places):
                    outs[c] = jnp.where(lane == (n + off) % LANES, turned, outs[c])
    cells = [
        x if c == 0 else pltpu.roll(x, (-(c if c < 3 else c - 6)) % LANES, axis=1)
        for c, x in enumerate(cells)
    ]

    def spread(x, off):
        x = pltpu.roll(x, (-off) % LANES, axis=1) if off else x
        x = x + pltpu.roll(x, 1, axis=1)
        return x + pltpu.roll(x, 2, axis=1)

    d_cols = [spread(x, off) for x, off in zip(d_cols, (0, 1, -2, -1))]
    v_cols = [spread(x, off) for x, off in zip(v_cols, (0, -2, -1))]
    s_cols = [spread(x, off) for x, off in zip(s_cols, (0, -2, -1))]
    level_of = lane // tracers

    def column_mask(c):
        col = bottom_v[:, c : c + 1] if c >= 0 else bottom_v[:, cols + c : cols + c + 1]
        ok = (level_of < jnp.broadcast_to(col, (rows, LANES))) & (lane < items)
        return jnp.where(ok, 1.0, 0.0)

    m = [column_mask(c) for c in (0, 1, 2, -3, -2, -1)]
    jump_01 = (cells[1] - cells[0]) * (m[0] * m[1])
    jump_12 = (cells[2] - cells[1]) * (m[1] * m[2])
    jump_e0 = (cells[4] - cells[3]) * (m[3] * m[4])
    jump_e1 = (cells[5] - cells[4]) * (m[4] * m[5])

    def pair(low, high):
        return low + pltpu.roll(high, 64, axis=1)

    odd_lon = lax.rem(lax.axis_index(lon_name), 2) == 1
    odd_lat = lax.rem(lax.axis_index(lat_name), 2) == 1
    east = (pair(cells[5], jump_e1), pair(d_cols[3], v_cols[2]), pair(s_cols[2], m[5]))
    west = (pair(cells[0], jump_01), pair(d_cols[0], zero), pair(zero, m[0]))
    for n in range(3):
        pay_c[n] = jnp.where(odd_lon, west[n], east[n])
        pay_d[n] = jnp.where(odd_lon, east[n], west[n])
    for n, x in enumerate(
        [cells[0], cells[1], jump_12, cells[4], cells[5], jump_e0] + d_cols + v_cols + s_cols
    ):
        own_lon[n] = x

    for b in range(items // ROWS):
        at = pl.ds(b * ROWS, ROWS)
        level = (sub + b * ROWS) // tracers
        m = [
            jnp.where(level < jnp.broadcast_to(x, (ROWS, cols)), 1.0, 0.0) for x in row_bottoms
        ]
        x = block[b]
        j01 = (x[1] - x[0]) * (m[0] * m[1])
        j12 = (x[2] - x[1]) * (m[1] * m[2])
        k0 = (x[4] - x[3]) * (m[3] * m[4])
        k1 = (x[5] - x[4]) * (m[4] * m[5])
        for n, y in enumerate((x[0], x[1], j12, x[4], x[5], k0)):
            own_lat[n, at, :] = y
        pay_a[at, :] = jnp.where(odd_lat, x[0], x[5])
        pay_b[at, :] = jnp.where(odd_lat, x[5], x[0])
        at = pl.ds(items + b * ROWS, ROWS)
        pay_a[at, :] = jnp.where(odd_lat, j01, k1)
        pay_b[at, :] = jnp.where(odd_lat, k1, j01)
    base = 2 * items
    for k in range(levels):
        values = (
            diff_v[k, 0:1, :],
            diff_v[k, 1:2, :],
            diff_v[k, rows - 2 : rows - 1, :],
            diff_v[k, rows - 1 : rows, :],
            north_v[0, k, 0:1, :],
            north_v[1, k, 6:7, :],
            north_v[1, k, 7:8, :],
            north_v[2, k, 0:1, :],
            north_v[3, k, 6:7, :],
            north_v[3, k, 7:8, :],
        )
        for n, y in enumerate(values):
            own_lat_coef[n, k : k + 1, :] = y
        for n, top in enumerate((values[3], values[6], values[9])):
            low = values[0] if n == 0 else jnp.zeros_like(top)
            r = base + n * levels + k
            pay_a[r : r + 1, :] = jnp.where(odd_lat, low, top)
            pay_b[r : r + 1, :] = jnp.where(odd_lat, top, low)
    r = base + 3 * levels
    low, top = row_bottoms[0].astype(F32), row_bottoms[5].astype(F32)
    pay_a[r : r + 1, :] = jnp.where(odd_lat, low, top)
    pay_b[r : r + 1, :] = jnp.where(odd_lat, top, low)
    for q in range(r + 1, pay_a.shape[0]):
        pay_a[q : q + 1, :] = jnp.zeros_like(low)
        pay_b[q : q + 1, :] = jnp.zeros_like(low)


def pack(tracer, east_vel, north_vel, diff, east_slope, north_slope, bottom):
    tracers, levels, rows, cols = tracer.shape
    items = tracers * levels
    lat_rows = -(-(2 * items + 3 * levels + 1) // ROWS) * ROWS
    shape = jax.ShapeDtypeStruct
    vmem = pl.BlockSpec(memory_space=pltpu.VMEM)

    def body(*refs):
        pack_kernel(levels, tracers, rows, cols, "lon", "lat", *refs)

    return pl.pallas_call(
        body,
        name="pack_edges",
        in_specs=[pl.BlockSpec(memory_space=pltpu.HBM)] * 7,
        out_specs=[vmem] * 7,
        out_shape=[
            shape((lat_rows, cols), F32),
            shape((lat_rows, cols), F32),
            shape((3, rows, LANES), F32),
            shape((3, rows, LANES), F32),
            shape((16, rows, LANES), F32),
            shape((6, items, cols), F32),
            shape((10, levels, cols), F32),
        ],
        scratch_shapes=[
            pltpu.VMEM((tracers, levels, rows, cols), F32),
            pltpu.VMEM((levels, rows, cols), F32),
            pltpu.VMEM((levels, rows, cols), F32),
            pltpu.VMEM((levels, rows, cols), F32),
            pltpu.VMEM((4, levels, ROWS, cols), F32),
            pltpu.VMEM((rows, cols), jnp.int32),
            pltpu.SemaphoreType.DMA((levels // 3, 4)),
            pltpu.SemaphoreType.DMA((5,)),
        ],
        compiler_params=pltpu.CompilerParams(vmem_limit_bytes=24 << 20),
        cost_estimate=pl.CostEstimate(flops=10**6, bytes_accessed=7 * 10**6, transcendentals=0),
    )(tracer, east_vel, north_vel, diff, east_slope, north_slope, bottom)


def interior_kernel(levels, tracers, rows, cols, *refs):
    (
        tracer,
        east_vel,
        north_vel,
        diff,
        east_slope,
        north_slope,
        bottom,
        explicit,
        ring,
        open_at,
        coef,
    ) = refs
    step = pl.program_id(0)
    blocks = rows // ROWS
    halves = (slice(0, LANES), slice(LANES, 2 * LANES))
    lane = iota((ROWS, LANES), 1)
    sub = iota((ROWS, LANES), 0)

    def chunk(b):
        return slice(b * ROWS, (b + 1) * ROWS)

    def east_of(x):
        left, right = x
        turned = pltpu.roll(right, LANES - 1, axis=1)
        return (
            jnp.where(lane == LANES - 1, turned, pltpu.roll(left, LANES - 1, axis=1)),
            turned,
        )

    def west_of(x):
        left, right = x
        turned = pltpu.roll(left, 1, axis=1)
        return turned, jnp.where(lane == 0, turned, pltpu.roll(right, 1, axis=1))

    def up(x):
        return tuple(pltpu.roll(y, ROWS - 1, axis=0) for y in x)

    def down(x):
        return tuple(pltpu.roll(y, 1, axis=0) for y in x)

    def north_of(turned, turned_next):
        if turned_next is None:
            return turned
        return tuple(jnp.where(sub == ROWS - 1, n, y) for y, n in zip(turned, turned_next))

    def south_of(turned, turned_before):
        if turned_before is None:
            return turned
        return tuple(jnp.where(sub == 0, n, y) for y, n in zip(turned, turned_before))

    def load(ref, *index):
        *lead, b = index
        return tuple(ref[(*lead, chunk(b), h)] for h in halves)

    @pl.when(step == 0)
    def _():
        ring[2] = jnp.zeros(ring.shape[1:], F32)
        for b in range(blocks):
            here = load(bottom, b)
            nxt = load(bottom, min(b + 1, blocks - 1))
            east = tuple(jnp.minimum(x, y) for x, y in zip(here, east_of(here)))
            north = tuple(
                jnp.minimum(x, y) for x, y in zip(here, north_of(up(here), up(nxt)))
            )
            row = sub + b * ROWS
            for i, h in enumerate(halves):
                col = lane + i * LANES
                open_at[0, chunk(b), h] = east[i]
                open_at[1, chunk(b), h] = jnp.where(
                    (col == 0) | (col >= cols - 2), 0, east[i]
                )
                open_at[2, chunk(b), h] = north[i]
                open_at[3, chunk(b), h] = jnp.where(
                    (row == 0) | (row >= rows - 2), 0, north[i]
                )

    @pl.when(step < levels)
    def _():
        slot = lax.rem(step, 3)
        for b in range(blocks):
            sea = tuple(x > step for x in load(bottom, b))
            for t in range(tracers):
                for i, h in enumerate(halves):
                    ring[slot, t, chunk(b), h] = jnp.where(sea[i], tracer[t, 0, chunk(b), h], 0.0)

    @pl.when(step == levels)
    def _():
        ring[levels % 3] = jnp.zeros(ring.shape[1:], F32)

    @pl.when(step > 0)
    def _():
        level = step - 1
        slot, above, below = lax.rem(step + 2, 3), lax.rem(step + 1, 3), lax.rem(step, 3)
        for b in range(blocks):
            here = load(diff, 0, b)
            north = north_of(up(here), up(load(diff, 0, min(b + 1, blocks - 1))))
            for way, other, vel, slope in (
                (0, east_of(here), east_vel, east_slope),
                (1, north, north_vel, north_slope),
            ):
                for i, h in enumerate(halves):
                    at = (chunk(b), h)
                    free = open_at[(2 * way, *at)] > level
                    face = open_at[(2 * way + 1, *at)] > level
                    speed = jnp.where(face, vel[(0, *at)], 0.0)
                    mean = jnp.where(face, 0.5 * (here[i] + other[i]), 0.0)
                    coef[(5 * way, *at)] = jnp.where(free, 1.0, 0.0)
                    coef[(5 * way + 1, *at)] = speed
                    coef[(5 * way + 2, *at)] = limiter_weight(speed)
                    coef[(5 * way + 3, *at)] = mean
                    coef[(5 * way + 4, *at)] = 0.125 * slope[(0, *at)] * mean

        def face(way, b, here, other, jump, bend, bend_other, tilt):
            out = []
            for i, h in enumerate(halves):
                at = (chunk(b), h)
                speed = coef[(5 * way + 1, *at)]
                ahead = speed >= 0
                upstream = jnp.where(ahead, here[i], other[i])
                limited = jnp.where(ahead, bend[i], bend_other[i])
                out.append(
                    (coef[(5 * way + 3, *at)] * jump[i] - coef[(5 * way + 4, *at)] * tilt[i])
                    - (speed * upstream + coef[(5 * way + 2, *at)] * limited)
                )
            return tuple(out)

        def sub2(x, y):
            return tuple(p - q for p, q in zip(x, y))

        def add2(x, y):
            return tuple(p + q for p, q in zip(x, y))

        def mul2(x, y):
            return tuple(p * q for p, q in zip(x, y))

        def one(t, carry):
            def stage(b):
                here = load(ring, slot, t, b)
                tilt = sub2(load(ring, below, t, b), load(ring, above, t, b))
                return here, up(here), tilt, up(tilt)

            now = stage(0)
            jump_before = bend_turned = flux_before = None
            held = None
            for b in range(blocks + 1):
                if b < blocks:
                    nxt = stage(b + 1) if b + 1 < blocks else (None,) * 4
                    here, turned, tilt, tilt_turned = now
                    north = north_of(turned, nxt[1])
                    step_n = sub2(north, here)
                    jump = mul2(step_n, load(coef, 5, b))
                    jump_turned = down(jump)
                    bend = tuple(
                        minmod(x, y) for x, y in zip(jump, south_of(jump_turned, jump_before))
                    )
                    bend_turned = up(bend)
                    jump_before = jump_turned
                if held is not None:
                    pb, p_here, p_north, p_step, p_bend, p_bend_turned, p_tilt, p_tilt_n = held
                    bend_n = north_of(p_bend_turned, bend_turned if b < blocks else None)
                    flux = face(
                        1, pb, p_here, p_north, p_step, p_bend, bend_n, add2(p_tilt, p_tilt_n)
                    )
                    flux_turned = down(flux)
                    if flux_before is None:
                        flux_s = tuple(jnp.where(sub == 0, 0.0, y) for y in flux_turned)
                    else:
                        flux_s = south_of(flux_turned, flux_before)
                    flux_before = flux_turned
                    total = add2(p_here, sub2(flux, flux_s))
                    east = east_of(p_here)
                    step_e = sub2(east, p_here)
                    jump_e = mul2(step_e, load(coef, 0, pb))
                    bend_e = tuple(minmod(x, y) for x, y in zip(jump_e, west_of(jump_e)))
                    flux_e = face(
                        0,
                        pb,
                        p_here,
                        east,
                        step_e,
                        bend_e,
                        east_of(bend_e),
                        add2(p_tilt, east_of(p_tilt)),
                    )
                    left, right = west_of(flux_e)
                    flux_w = (jnp.where(lane == 0, 0.0, left), right)
                    total = add2(total, sub2(flux_e, flux_w))
                    for i, h in enumerate(halves):
                        explicit[t, 0, chunk(pb), h] = total[i]
                if b < blocks:
                    tilt_n = north_of(tilt_turned, nxt[3])
                    held = (b, here, north, step_n, bend, bend_turned, tilt, tilt_n)
                    now = nxt
            return carry

        lax.fori_loop(0, tracers, one, 0)


def interior(tracer, east_vel, north_vel, diff, east_slope, north_slope, bottom):
    tracers, levels, rows, cols = tracer.shape

    def body(*refs):
        interior_kernel(levels, tracers, rows, cols, *refs)

    flat = pl.BlockSpec((1, rows, cols), lambda s: (jnp.maximum(s - 1, 0), 0, 0))
    return pl.pallas_call(
        body,
        name="interior_faces",
        grid=(levels + 1,),
        in_specs=[
            pl.BlockSpec(
                (tracers, 1, rows, cols), lambda s: (0, jnp.minimum(s, levels - 1), 0, 0)
            ),
            flat,
            flat,
            flat,
            flat,
            flat,
            pl.BlockSpec((rows, cols), lambda s: (0, 0)),
        ],
        out_specs=pl.BlockSpec(
            (tracers, 1, rows, cols), lambda s: (0, jnp.maximum(s - 1, 0), 0, 0)
        ),
        out_shape=jax.ShapeDtypeStruct(tracer.shape, F32),
        scratch_shapes=[
            pltpu.VMEM((3, tracers, rows, cols), F32),
            pltpu.VMEM((4, rows, cols), jnp.int32),
            pltpu.VMEM((10, rows, cols), F32),
        ],
        compiler_params=pltpu.CompilerParams(
            dimension_semantics=("arbitrary",), vmem_limit_bytes=16 << 20
        ),
        cost_estimate=pl.CostEstimate(
            flops=60 * tracer.size, bytes_accessed=12 * 10**6, transcendentals=0
        ),
    )(tracer, east_vel, north_vel, diff, east_slope, north_slope, bottom)


def edge_faces(m1, m2, m3, j0, j3, open1, open2, d1, d2, d3, v0, v1, s0, s1, tilt):
    j1 = (m2 - m1) * open1
    j2 = (m3 - m2) * open2
    t1, t2, t3 = tilt(m1), tilt(m2), tilt(m3)

    def face(low, high, behind, jump, ahead, opened, d_sum, vel, slope, tilts):
        speed = vel * opened
        forward = speed >= 0
        flux = speed * jnp.where(forward, low, high) + limiter_weight(speed) * minmod(
            jump, jnp.where(forward, behind, ahead)
        )
        return 0.5 * d_sum * (jump - 0.125 * slope * opened * tilts) - flux

    return (
        face(m1, m2, j0, j1, j2, open1, d1 + d2, v0, s0, t1 + t2),
        face(m2, m3, j1, j2, j3, open2, d2 + d3, v1, s1, t2 + t3),
    )


def solve_kernel(levels, tracers, rows, cols, lon_name, lat_name, lat_count, *refs):
    (
        explicit,
        vertical,
        bottom,
        got_a,
        got_b,
        got_c,
        got_d,
        own_lon,
        own_lat,
        own_lat_coef,
        out,
        fix_lon,
        fix_lat,
        south,
        north,
        pivots,
        solved,
    ) = refs
    step = pl.program_id(0)
    blocks = rows // ROWS
    items = levels * tracers
    base = 2 * items
    halves = (slice(0, LANES), slice(LANES, 2 * LANES))
    lane = iota((ROWS, LANES), 1)
    sub = iota((ROWS, LANES), 0)

    @pl.when(step == 0)
    def _():
        odd_lon = lax.rem(lax.axis_index(lon_name), 2) == 1
        lat = lax.axis_index(lat_name)
        odd_lat = lax.rem(lat, 2) == 1
        top = lat == lat_count - 1
        item = iota((ROWS, LANES), 1)
        inside = item < items
        level = item // tracers

        def tilt_lanes(x):
            return pltpu.roll(x, LANES - tracers, axis=1) - pltpu.roll(x, tracers, axis=1)

        for b in range(blocks):
            at = slice(b * ROWS, (b + 1) * ROWS)

            def mask(c):
                col = jnp.broadcast_to(bottom[at, c : c + 1], (ROWS, LANES))
                return jnp.where((level < col) & inside, 1.0, 0.0)

            def halves_of(pays):
                low, high = [], []
                for x in pays:
                    low.append(jnp.where(inside, x, 0.0))
                    high.append(jnp.where(inside, pltpu.roll(x, 64, axis=1), 0.0))
                return low, high

            c_got = [got_c[n, at, :] for n in range(3)]
            d_got = [got_d[n, at, :] for n in range(3)]
            from_west = [jnp.where(odd_lon, c, d) for c, d in zip(c_got, d_got)]
            from_east = [jnp.where(odd_lon, d, c) for c, d in zip(c_got, d_got)]
            own = [own_lon[n, at, :] for n in range(16)]
            (wm, wd, ws), (wj, wv, wk) = halves_of(from_west)
            m0, m1 = mask(0), mask(1)
            f0, f1 = edge_faces(
                wm, own[0], own[1], wj, own[2], wk * m0, m0 * m1,
                wd, own[6], own[7], wv, own[10], ws, own[13], tilt_lanes,
            )
            fix_lon[0, at, :] = (f1 - f0) * m0
            fix_lon[1, at, :] = -f1 * m1
            (em, ed, _), (ej, _, ek) = halves_of(from_east)
            m0, m1 = mask(cols - 2), mask(cols - 1)
            f0, f1 = edge_faces(
                own[3], own[4], em, own[5], ej, m0 * m1, m1 * ek,
                own[8], own[9], ed, own[11], own[12], own[14], own[15], tilt_lanes,
            )
            fix_lon[2, at, :] = f0 * m0
            fix_lon[3, at, :] = (f1 - f0) * m1

        south[...] = jnp.where(odd_lat, got_a[...], got_b[...])

        @pl.when(jnp.logical_not(top))
        def _():
            north[...] = jnp.where(odd_lat, got_b[...], got_a[...])

        @pl.when(top)
        def _():
            for b in range(north.shape[0] // ROWS):
                at = slice(b * ROWS, (b + 1) * ROWS)
                for i in range(2):
                    x = got_b[at, halves[1 - i]]
                    for bit in range(7):
                        size = 1 << bit
                        x = jnp.where(
                            (lane & size) != 0,
                            pltpu.roll(x, size, axis=1),
                            pltpu.roll(x, LANES - size, axis=1),
                        )
                    north[at, halves[i]] = x

        wide = iota((ROWS, cols), 0)
        sign = jnp.where(top, -1.0, 1.0)

        def spread_rows(ref, first, b):
            k = b * ROWS // tracers
            low, high = ref[first + k : first + k + 1, :], ref[first + k + 1 : first + k + 2, :]
            return jnp.where(
                wide < tracers,
                jnp.broadcast_to(low, (ROWS, cols)),
                jnp.broadcast_to(high, (ROWS, cols)),
            )

        def tilt_rows_of(read):
            def tilt(b):
                here = read(b)
                zeros = jnp.zeros_like(here)
                turned = pltpu.roll(here, tracers, axis=0)
                after = pltpu.roll(read(b + 1), tracers, axis=0) if b + 1 < items // ROWS else zeros
                before = pltpu.roll(read(b - 1), tracers, axis=0) if b else zeros
                return jnp.where(wide < tracers, turned, after) - jnp.where(
                    wide < tracers, before, turned
                )

            return tilt

        def own_row(n):
            return lambda b: own_lat[n, b * ROWS : (b + 1) * ROWS, :]

        def ghost_row(ref):
            return lambda b: ref[b * ROWS : (b + 1) * ROWS, :]

        for b in range(items // ROWS):
            at = slice(b * ROWS, (b + 1) * ROWS)
            past = slice(items + b * ROWS, items + (b + 1) * ROWS)
            level = (wide + b * ROWS) // tracers

            def mask(row):
                return jnp.where(level < jnp.broadcast_to(row, (ROWS, cols)), 1.0, 0.0)

            def coef(n):
                return spread_rows(own_lat_coef.at[n], 0, b)

            def ghost_mask(ref):
                row = ref[base + 3 * levels : base + 3 * levels + 1, :]
                return jnp.where(level.astype(F32) < jnp.broadcast_to(row, (ROWS, cols)), 1.0, 0.0)

            def run(reads, j0, j3, open1, open2, d, v, s):
                tilts = [tilt_rows_of(r)(b) for r in reads]
                values = [r(b) for r in reads]
                lookup = dict(zip(map(id, values), tilts))
                return edge_faces(*values, j0, j3, open1, open2, *d, *v, *s,
                                  lambda x: lookup[id(x)])

            m0, m1 = mask(bottom[0:1, :]), mask(bottom[1:2, :])
            f0, f1 = run(
                (ghost_row(south), own_row(0), own_row(1)),
                south[past, :], own_lat[2, at, :], ghost_mask(south) * m0, m0 * m1,
                (spread_rows(south, base, b), coef(0), coef(1)),
                (spread_rows(south, base + levels, b), coef(4)),
                (spread_rows(south, base + 2 * levels, b), coef(7)),
            )
            fix_lat[0, at, :] = (f1 - f0) * m0
            fix_lat[1, at, :] = -f1 * m1
            m0 = mask(bottom[rows - 2 : rows - 1, :])
            m1 = mask(bottom[rows - 1 : rows, :])
            top_vel = coef(6)
            ghost_vel = spread_rows(north, base + levels, b)
            top_vel = jnp.where(top, 0.5 * (top_vel - ghost_vel), top_vel)
            f0, f1 = run(
                (own_row(3), own_row(4), ghost_row(north)),
                own_lat[5, at, :], sign * north[past, :], m0 * m1, m1 * ghost_mask(north),
                (coef(2), coef(3), spread_rows(north, base, b)),
                (coef(5), top_vel),
                (coef(8), coef(9)),
            )
            fix_lat[2, at, :] = f0 * m0
            fix_lat[3, at, :] = (f1 - f0) * m1

    depth = tuple(bottom[pl.ds(pl.multiple_of(step * ROWS, ROWS), ROWS), h] for h in halves)
    for i, h in enumerate(halves):
        ratio = above = None
        for k in range(levels):
            if k + 1 < levels:
                below = jnp.where(depth[i] > k + 1, vertical[k, :, h], 0.0)
            if k == 0:
                pivot = 1.0 + below
            elif k + 1 < levels:
                pivot = (1.0 + above + below) + above * ratio
            else:
                pivot = (1.0 + above) + above * ratio
            inverse = 1.0 / pivot
            pivots[0, k, :, h] = inverse
            if k:
                pivots[1, k, :, h] = above
            if k + 1 < levels:
                ratio = below * inverse
                pivots[2, k, :, h] = ratio
                above = below

    first_block = step == 0
    last_block = step == blocks - 1
    row0 = jnp.where(first_block, 0, ROWS - 2)
    pick = jnp.where(first_block, 0, 2)

    @pl.when(first_block | last_block)
    def _():
        for t in range(tracers):
            for k in range(levels):
                n = k * tracers + t
                for i, h in enumerate(halves):
                    low = fix_lat[pick, n : n + 1, h]
                    high = fix_lat[pick + 1, n : n + 1, h]
                    explicit_fix = jnp.where(
                        sub == row0,
                        jnp.broadcast_to(low, (ROWS, LANES)),
                        jnp.where(
                            sub == row0 + 1, jnp.broadcast_to(high, (ROWS, LANES)), 0.0
                        ),
                    )
                    solved[t, k, :, h] = explicit_fix

    @pl.when(jnp.logical_not(first_block | last_block))
    def _():
        solved[...] = jnp.zeros(solved.shape, F32)

    at = pl.ds(pl.multiple_of(step * ROWS, ROWS), ROWS)
    fixes = [fix_lon[n, at, :] for n in range(4)]
    for t in range(tracers):
        for i, h in enumerate(halves):
            a, b = fixes[2 * i], fixes[2 * i + 1]
            at_a, at_b = (0, 1) if i == 0 else (LANES - 2, LANES - 1)
            values = []
            value = None
            for k in range(levels):
                n = k * tracers + t
                patch = jnp.where(
                    lane == at_a,
                    pltpu.roll(a, (at_a - n) % LANES, axis=1),
                    jnp.where(lane == at_b, pltpu.roll(b, (at_b - n) % LANES, axis=1), 0.0),
                )
                right = (explicit[t, k, :, h] + solved[t, k, :, h]) + patch
                right = jnp.where(depth[i] > k, right, 0.0)
                if k:
                    right = right + pivots[1, k, :, h] * value
                value = right * pivots[0, k, :, h]
                values.append(value)
            nxt = values[-1]
            out[t, levels - 1, :, h] = nxt
            for k in range(levels - 2, -1, -1):
                nxt = values[k] + pivots[2, k, :, h] * nxt
                out[t, k, :, h] = nxt


def solve(explicit, vertical, bottom, got, own):
    tracers, levels, rows, cols = explicit.shape
    items = levels * tracers
    lat_rows = got[0].shape[0]
    lat_count = lax.axis_size("lat")

    def body(*refs):
        solve_kernel(levels, tracers, rows, cols, "lon", "lat", lat_count, *refs)

    whole = [
        pl.BlockSpec(x.shape, lambda s, n=x.ndim: (0,) * n, pipeline_mode=pl.Buffered(1))
        for x in (bottom, *got, *own)
    ]
    block = pl.BlockSpec((tracers, levels, ROWS, cols), lambda s: (0, 0, s, 0))
    return pl.pallas_call(
        body,
        name="edges_and_solve",
        grid=(rows // ROWS,),
        in_specs=[block, pl.BlockSpec((levels - 1, ROWS, cols), lambda s: (0, s, 0)), *whole],
        out_specs=block,
        out_shape=jax.ShapeDtypeStruct(explicit.shape, F32),
        scratch_shapes=[
            pltpu.VMEM((4, rows, LANES), F32),
            pltpu.VMEM((4, items, cols), F32),
            pltpu.VMEM((lat_rows, cols), F32),
            pltpu.VMEM((lat_rows, cols), F32),
            pltpu.VMEM((3, levels, ROWS, cols), F32),
            pltpu.VMEM((tracers, levels, ROWS, cols), F32),
        ],
        compiler_params=pltpu.CompilerParams(
            dimension_semantics=("arbitrary",), vmem_limit_bytes=16 << 20
        ),
        cost_estimate=pl.CostEstimate(
            flops=20 * explicit.size, bytes_accessed=8 * 10**6, transcendentals=0
        ),
    )(explicit, vertical, bottom, *got, *own)


def local(
    tracer,
    east_velocity,
    north_velocity,
    diffusivity,
    east_slope,
    north_slope,
    vertical_diffusivity,
    sea_mask,
    bottom,
):
    lon, lat = lax.axis_size("lon"), lax.axis_size("lat")
    args = (tracer, east_velocity, north_velocity, diffusivity, east_slope, north_slope, bottom)
    pay_a, pay_b, pay_c, pay_d, *own = pack(*args)

    def swap(pairs):
        return [p for a, b in pairs for p in ((a, b), (b, a))]

    def at(i, j):
        return i * lat + j

    near_lat = swap([(j, j + 1) for j in range(0, lat, 2)])
    far_lat = swap([(at(i, j), at(i, j + 1)) for i in range(lon) for j in range(1, lat - 1, 2)])
    far_lat += [(at(i, lat - 1), at(lon - 1 - i, lat - 1)) for i in range(lon)]
    near_lon = swap([(i, i + 1) for i in range(0, lon, 2)])
    far_lon = swap([(i, (i + 1) % lon) for i in range(1, lon, 2)])
    got_a = lax.ppermute(pay_a, "lat", near_lat)
    got_c = lax.ppermute(pay_c, "lon", near_lon)
    got_b = lax.ppermute(pay_b, ("lon", "lat"), far_lat)
    got_d = lax.ppermute(pay_d, "lon", far_lon)
    explicit = interior(*args)
    return solve(
        explicit, vertical_diffusivity, bottom, (got_a, got_b, got_c, got_d), tuple(own)
    )


def solution(mesh):
    field = P(None, "lat", "lon")
    placed = (
        P(None, None, "lat", "lon"),
        field,
        field,
        field,
        field,
        field,
        field,
        field,
        P("lat", "lon"),
    )
    return jax.shard_map(
        local, mesh=mesh, in_specs=placed, out_specs=P(None, None, "lat", "lon"), check_vma=False
    )
```

profile of v0, /device:TPU:4, one launch (start us, length us, event | category | flops | bytes accessed | tf_op | source)
XLA Modules:
  0.0 50.5 jit_solution(16544474512827221071)
XLA Ops:
  0.0 0.0 copy-start
  0.0 1.9 %copy-done = f32[4,12,64,256]{3,2,1,0:T(8,128)S(1)} copy-done((f32[4,12,64,256]{3,2,1,0:T(8,128)S(1)}, f32[4,12,64,256]{3,2,1,0:T(8,128)}, u32[]{:S(2)}) %copy-start) | copy-done | bytes 3145752
  1.9 0.0 copy-start.2
  1.9 1.1 %copy-done.2 = f32[12,64,256]{2,1,0:T(8,128)S(1)} copy-done((f32[12,64,256]{2,1,0:T(8,128)S(1)}, f32[12,64,256]{2,1,0:T(8,128)}, u32[]{:S(2)}) %copy-start.2) | copy-done | bytes 786456
  3.0 0.0 copy-start.3
  3.0 1.1 %copy-done.3 = f32[12,64,256]{2,1,0:T(8,128)S(1)} copy-done((f32[12,64,256]{2,1,0:T(8,128)S(1)}, f32[12,64,256]{2,1,0:T(8,128)}, u32[]{:S(2)}) %copy-start.3) | copy-done | bytes 786456
  4.2 0.0 copy-start.4
  4.2 1.1 %copy-done.4 = f32[12,64,256]{2,1,0:T(8,128)S(1)} copy-done((f32[12,64,256]{2,1,0:T(8,128)S(1)}, f32[12,64,256]{2,1,0:T(8,128)}, u32[]{:S(2)}) %copy-start.4) | copy-done | bytes 786456
  5.3 1.1 %copy-done.5 = f32[12,64,256]{2,1,0:T(8,128)S(1)} copy-done((f32[12,64,256]{2,1,0:T(8,128)S(1)}, f32[12,64,256]{2,1,0:T(8,128)}, u32[]{:S(2)}) %copy-start.5) | copy-done | bytes 786456
  6.4 1.1 %copy-done.6 = f32[12,64,256]{2,1,0:T(8,128)S(1)} copy-done((f32[12,64,256]{2,1,0:T(8,128)S(1)}, f32[12,64,256]{2,1,0:T(8,128)}, u32[]{:S(2)}) %copy-start.6) | copy-done | bytes 786456
  7.6 0.8 %copy-done.8 = s32[64,256]{1,0:T(8,128)S(1)} copy-done((s32[64,256]{1,0:T(8,128)S(1)}, s32[64,256]{1,0:T(8,128)}, u32[]{:S(2)}) %copy-start.8) | copy-done | bytes 65560
  8.4 6.3 %pack_edges.1 = (f32[136,256]{1,0:T(8,128)S(1)}, f32[136,256]{1,0:T(8,128)S(1)}, f32[3,64,128]{2,1,0:T(8,128)S(1)}, f32[3,64,128]{2,1,0:T(8,128)S(1)}, f32[16,64...) custom-call(f32[4,12,64,256]{3,2,1,0:T(8,128)S(1)} %copy-done, ...), custom_call_target="tpu_custom_call" | custom-call | flops 1000000 | bytes 7000000 | tf_op jit(solution)/shard_map/pack_edges/pallas_call | solution.py:230
  14.8 0.1 collective-permute-start
  14.9 5.0 %collective-permute-start.1 = (f32[136,256]{1,0:T(8,128)S(1)}, f32[136,256]{1,0:T(8,128)S(1)}, u32[]{:S(2)}, u32[]{:S(2)}) collective-permute-start(f32[136,256]{1,0:T(8,128)S(1)} %get-tuple-element.13), channel_id=1, source_target_pairs={{1,2},{2,1},{3,4},{4,3},{5,6},{6,5},{7,8},{8,7},{9,10},{10,9},{11,... | collective-permute-start | bytes 417800 | tf_op jit(solution)/shard_map/ppermute | solution.py:835
  19.8 2.2 %collective-permute-start.2 = (f32[3,64,128]{2,1,0:T(8,128)S(1)}, f32[3,64,128]{2,1,0:T(8,128)S(1)}, u32[]{:S(2)}, u32[]{:S(2)}) collective-permute-start(f32[3,64,128]{2,1,0:T(8,128)S(1)} %get-tuple-element.14), channel_id=1, source_target_pairs={{0,16},{16,0},{32,48},{48,32},{64,80},{80,64},{96,112},{112,96},{1... | collective-permute-start | bytes 294920 | tf_op jit(solution)/shard_map/ppermute | solution.py:834
  22.0 5.4 %collective-permute-start.3 = (f32[3,64,128]{2,1,0:T(8,128)S(1)}, f32[3,64,128]{2,1,0:T(8,128)S(1)}, u32[]{:S(2)}, u32[]{:S(2)}) collective-permute-start(f32[3,64,128]{2,1,0:T(8,128)S(1)} %get-tuple-element.15), channel_id=1, source_target_pairs={{16,32},{32,16},{48,64},{64,48},{80,96},{96,80},{112,128},{128,112... | collective-permute-start | bytes 294920 | tf_op jit(solution)/shard_map/ppermute | solution.py:836
  27.4 0.0 copy-done.1
  27.4 16.9 %interior_faces.1.refs_0_ = f32[4,12,64,256]{3,2,1,0:T(8,128)S(1)} custom-call(f32[4,12,64,256]{3,2,1,0:T(8,128)S(1)} %copy-done.1, f32[12,64,256]{2,1,0:T(8,128)S(1)} %copy-done.2, f32[12,64,256]{2,1,0:T(8,128)S(1)} %copy-done.3, f32[12,64,256]{2,1,0:T(8,128)S(1)} %copy-done.4, f32[12,64,256]{2,1,0:T(8,128)S(1)} %copy-done.5, f32[12,64,256]{2,1,0:T(8,128)S(1)} %copy-done.6, ...), custom_call_target="tpu_custom_call" | custom-call | flops 47185920 | bytes 12000000 | tf_op jit(solution)/shard_map/interior_faces/pallas_call | solution.py:466
  44.4 0.0 collective-permute-done.2.refs_5_
  44.4 0.0 collective-permute-done.3.refs_6_
  44.4 0.0 collective-permute-done.refs_3_
  44.4 0.0 collective-permute-done.1.refs_4_
  44.4 0.0 copy-done.7
  44.4 6.1 %edges_and_solve.1 = f32[4,12,64,256]{3,2,1,0:T(8,128)} custom-call(f32[4,12,64,256]{3,2,1,0:T(8,128)S(1)} %interior_faces.1.refs_0_, f32[11,64,256]{2,1,0:T(8,128)S(1)} %copy-done.7, s32[64,256]{1,0:T(8,128)S(1)} %copy-done.8, f32[136,256]{1,0:T(8,128)S(1)} %collective-permute-done.refs_3_, f32[136,256]{1,0:T(8,128)S(1)} %collective-permute-done.1.refs_4_, ...), custom_call_target="tpu_custom_call" | custom-call | flops 15728640 | bytes 8000000 | tf_op jit(solution)/shard_map/edges_and_solve/pallas_call | solution.py:783
  (5 shorter events, 0.0 us)
Async XLA Ops:
  0.0 1.9 %copy-start = (f32[4,12,64,256]{3,2,1,0:T(8,128)S(1)}, f32[4,12,64,256]{3,2,1,0:T(8,128)}, u32[]{:S(2)}) copy-start(f32[4,12,64,256]{3,2,1,0:T(8,128)} %refs_0_.3) | copy-start | bytes 9437188
  1.9 1.1 %copy-start.2 = (f32[12,64,256]{2,1,0:T(8,128)S(1)}, f32[12,64,256]{2,1,0:T(8,128)}, u32[]{:S(2)}) copy-start(f32[12,64,256]{2,1,0:T(8,128)} %refs_1_.4) | copy-start | bytes 2359300
  3.0 1.1 %copy-start.3 = (f32[12,64,256]{2,1,0:T(8,128)S(1)}, f32[12,64,256]{2,1,0:T(8,128)}, u32[]{:S(2)}) copy-start(f32[12,64,256]{2,1,0:T(8,128)} %refs_2_.4) | copy-start | bytes 2359300
  4.2 1.1 %copy-start.4 = (f32[12,64,256]{2,1,0:T(8,128)S(1)}, f32[12,64,256]{2,1,0:T(8,128)}, u32[]{:S(2)}) copy-start(f32[12,64,256]{2,1,0:T(8,128)} %refs_3_.3) | copy-start | bytes 2359300
  5.3 1.1 %copy-start.5 = (f32[12,64,256]{2,1,0:T(8,128)S(1)}, f32[12,64,256]{2,1,0:T(8,128)}, u32[]{:S(2)}) copy-start(f32[12,64,256]{2,1,0:T(8,128)} %refs_4_.3) | copy-start | bytes 2359300
  6.4 1.1 %copy-start.6 = (f32[12,64,256]{2,1,0:T(8,128)S(1)}, f32[12,64,256]{2,1,0:T(8,128)}, u32[]{:S(2)}) copy-start(f32[12,64,256]{2,1,0:T(8,128)} %refs_5_.3) | copy-start | bytes 2359300
  7.6 0.8 %copy-start.8 = (s32[64,256]{1,0:T(8,128)S(1)}, s32[64,256]{1,0:T(8,128)}, u32[]{:S(2)}) copy-start(s32[64,256]{1,0:T(8,128)} %refs_2_.5) | copy-start | bytes 196612
  8.4 19.0 %copy-start.1 = (f32[4,12,64,256]{3,2,1,0:T(8,128)S(1)}, f32[4,12,64,256]{3,2,1,0:T(8,128)}, u32[]{:S(2)}) copy-start(f32[4,12,64,256]{3,2,1,0:T(8,128)} %refs_0_.3) | copy-start | bytes 9437188
  14.8 29.6 %collective-permute-start = (f32[136,256]{1,0:T(8,128)S(1)}, f32[136,256]{1,0:T(8,128)S(1)}, u32[]{:S(2)}, u32[]{:S(2)}) collective-permute-start(f32[136,256]{1,0:T(8,128)S(1)} %get-tuple-element.12), channel_id=1, source_target_pairs={{0,1},{1,0},{2,3},{3,2},{4,5},{5,4},{6,7},{7,6},{8,9},{9,8},{10,11... | collective-permute-start | bytes 417800 | tf_op jit(solution)/shard_map/ppermute | solution.py:833
  14.9 29.5 %collective-permute-start.1 = (f32[136,256]{1,0:T(8,128)S(1)}, f32[136,256]{1,0:T(8,128)S(1)}, u32[]{:S(2)}, u32[]{:S(2)}) collective-permute-start(f32[136,256]{1,0:T(8,128)S(1)} %get-tuple-element.13), channel_id=1, source_target_pairs={{1,2},{2,1},{3,4},{4,3},{5,6},{6,5},{7,8},{8,7},{9,10},{10,9},{11,... | collective-permute-start | bytes 417800 | tf_op jit(solution)/shard_map/ppermute | solution.py:835
  19.8 24.5 %collective-permute-start.2 = (f32[3,64,128]{2,1,0:T(8,128)S(1)}, f32[3,64,128]{2,1,0:T(8,128)S(1)}, u32[]{:S(2)}, u32[]{:S(2)}) collective-permute-start(f32[3,64,128]{2,1,0:T(8,128)S(1)} %get-tuple-element.14), channel_id=1, source_target_pairs={{0,16},{16,0},{32,48},{48,32},{64,80},{80,64},{96,112},{112,96},{1... | collective-permute-start | bytes 294920 | tf_op jit(solution)/shard_map/ppermute | solution.py:834
  22.0 22.4 %copy-start.7 = (f32[11,64,256]{2,1,0:T(8,128)S(1)}, f32[11,64,256]{2,1,0:T(8,128)}, u32[]{:S(2)}) copy-start(f32[11,64,256]{2,1,0:T(8,128)} %refs_1_.5) | copy-start | bytes 2162692
  22.0 22.4 %collective-permute-start.3 = (f32[3,64,128]{2,1,0:T(8,128)S(1)}, f32[3,64,128]{2,1,0:T(8,128)S(1)}, u32[]{:S(2)}, u32[]{:S(2)}) collective-permute-start(f32[3,64,128]{2,1,0:T(8,128)S(1)} %get-tuple-element.15), channel_id=1, source_target_pairs={{16,32},{32,16},{48,64},{64,48},{80,96},{96,80},{112,128},{128,112... | collective-permute-start | bytes 294920 | tf_op jit(solution)/shard_map/ppermute | solution.py:836
where the time goes:
time: 50.9 us; the launch traced here: 50.5 us
  Pallas kernels  29.4 us (58%)
  starting transfers between devices  12.6 us (25%)
  local copies, waits for them, and re-layouts  8.4 us (17%)
    pallas_call x1, Pallas kernels, interior(): pl.pallas_call(body, name='interior_faces', grid=(levels + 1,), in_specs=...  16.9 us
    unnamed x18, local copies, waits for them, and re-layouts  8.4 us
    pallas_call x1, Pallas kernels, pack(): pl.pallas_call(body, name='pack_edges', in_specs=[pl.BlockSpec(memory_spa...  6.34 us
    pallas_call x1, Pallas kernels, solve(): pl.pallas_call(body, name='edges_and_solve', grid=(rows // ROWS,), in_spe...  6.07 us
    ppermute x1, starting transfers between devices, local(): got_d = lax.ppermute(pay_d, 'lon', far_lon)  5.4 us
    ppermute x1, starting transfers between devices, local(): got_b = lax.ppermute(pay_b, ('lon', 'lat'), far_lat)  4.96 us
    ppermute x1, starting transfers between devices, local(): got_c = lax.ppermute(pay_c, 'lon', near_lon)  2.18 us
  transfers between devices with their start and end apart: 4, of which 0 were waited for; matrix products, arithmetic and copies ran while one was open for 0% of the time, Pallas kernels for 34%

commit v1 on v0

v1 whole, which is shorter than its diff:
```python
import jax
import jax.numpy as jnp
from jax import lax
from jax.experimental import pallas as pl
from jax.experimental.pallas import tpu as pltpu
from jax.sharding import PartitionSpec as P

F32 = jnp.float32
LANES = 128
ROWS = 8
VMEM_LIMIT = 61 << 20
SOLVE_LIMIT = 32 << 20


def iota(shape, dim):
    return lax.broadcasted_iota(jnp.int32, shape, dim)


def minmod(first, second):
    return jnp.minimum(
        jnp.maximum(second, jnp.minimum(first, 0.0)), jnp.maximum(first, 0.0)
    )


def limiter_weight(speed):
    size = jnp.abs(speed)
    return 0.5 * size * (1.0 - size)


def pack_kernel(levels, tracers, rows, cols, lon_name, lat_name, *refs):
    (
        tracer_hbm,
        east_vel_hbm,
        north_vel_hbm,
        diff_hbm,
        east_slope_hbm,
        north_slope_hbm,
        bottom_hbm,
        pay_a,
        pay_b,
        pay_c,
        pay_d,
        own_lon,
        own_lat,
        own_lat_coef,
        tracer_v,
        east_vel_v,
        diff_v,
        east_slope_v,
        north_v,
        bottom_v,
        sems,
        row_sems,
    ) = refs
    items = levels * tracers
    group = 3
    groups = levels // group
    last = rows - ROWS
    copies = []
    row_copies = [pltpu.make_async_copy(bottom_hbm, bottom_v, row_sems.at[0])]
    for n, (src, start) in enumerate(
        ((north_vel_hbm, 0), (north_vel_hbm, last), (north_slope_hbm, 0), (north_slope_hbm, last))
    ):
        row_copies.append(
            pltpu.make_async_copy(
                src.at[:, pl.ds(start, ROWS), :], north_v.at[n], row_sems.at[n + 1]
            )
        )
    for g in range(groups):
        span = pl.ds(g * group, group)
        fetch = [
            pltpu.make_async_copy(
                tracer_hbm.at[:, span], tracer_v.at[:, span], sems.at[g, 0]
            )
        ]
        for n, (src, dst) in enumerate(
            ((diff_hbm, diff_v), (east_vel_hbm, east_vel_v), (east_slope_hbm, east_slope_v))
        ):
            fetch.append(pltpu.make_async_copy(src.at[span], dst.at[span], sems.at[g, n + 1]))
        copies.append(fetch)
    for copy in copies[0]:
        copy.start()
    for copy in row_copies:
        copy.start()
    for fetch in copies[1:]:
        for copy in fetch:
            copy.start()

    lane = iota((rows, LANES), 1)
    couple = lane // 2
    even = lane % 2 == 0
    left_side = lane < 64
    sub = iota((ROWS, cols), 0)
    right = cols - LANES
    zero = jnp.zeros((rows, LANES), F32)
    first_two = second = third_last = last_two = zero
    coefs = [[zero, zero] for _ in range(3)]
    row_at = (0, 1, 2, rows - 3, rows - 2, rows - 1)
    for copy in row_copies:
        copy.wait()
    row_bottoms = [bottom_v[r : r + 1, :] for r in row_at]
    block = [[jnp.zeros((ROWS, cols), F32)] * 6 for _ in range(items // ROWS)]
    edge_bottom = jnp.where(left_side, bottom_v[:, :LANES], bottom_v[:, right:])

    def turn(x, by):
        by = by % LANES
        return pltpu.roll(x, by, axis=1) if by else x

    for g in range(groups):
        for copy in copies[g]:
            copy.wait()
        for k in range(g * group, (g + 1) * group):
            sea = edge_bottom > k
            for t in range(tracers):
                n = k * tracers + t
                both = jnp.where(
                    left_side, tracer_v[t, k, :, :LANES], tracer_v[t, k, :, right:]
                )
                turned = turn(jnp.where(sea, both, 0.0), 2 * n)
                first_two = jnp.where(couple == n, turned, first_two)
                last_two = jnp.where(couple == (n - 1) % 64, turned, last_two)
                second = jnp.where(lane == 2 * n + 2, turned, second)
                third_last = jnp.where(lane == (2 * n - 3) % LANES, turned, third_last)
                for c, r in enumerate(row_at):
                    block[n // ROWS][c] = jnp.where(
                        sub == n % ROWS,
                        jnp.broadcast_to(tracer_v[t, k, r : r + 1, :], (ROWS, cols)),
                        block[n // ROWS][c],
                    )
            n = k * tracers
            for ref, outs in zip((diff_v, east_vel_v, east_slope_v), coefs):
                turned = turn(jnp.where(left_side, ref[k, :, :LANES], ref[k, :, right:]), 2 * n)
                outs[0] = jnp.where(couple == n, turned, outs[0])
                outs[1] = jnp.where(couple == (n - 1) % 64, turned, outs[1])
    cells = [
        first_two, turn(first_two, -1), turn(second, -2),
        turn(third_last, 3), turn(last_two, 2), turn(last_two, 1),
    ]
    head = lane % (2 * tracers) == 0

    def spread(x, by):
        x = jnp.where(head, turn(x, by), 0.0)
        x = x + turn(x, 2)
        return x + turn(x, 4)

    d_cols = [spread(coefs[0][i], by) for i, by in ((0, 0), (0, -1), (1, 2), (1, 1))]
    v_cols, s_cols = (
        [spread(pair[i], by) for i, by in ((0, 0), (1, 2), (1, 1))] for pair in coefs[1:]
    )
    level_of = couple // tracers
    inside = couple < items

    def column_mask(c):
        col = bottom_v[:, c : c + 1] if c >= 0 else bottom_v[:, cols + c : cols + c + 1]
        ok = (level_of < jnp.broadcast_to(col, (rows, LANES))) & inside
        return jnp.where(ok, 1.0, 0.0)

    m = [column_mask(c) for c in (0, 1, 2, -3, -2, -1)]
    jump_01 = (cells[1] - cells[0]) * (m[0] * m[1])
    jump_12 = (cells[2] - cells[1]) * (m[1] * m[2])
    jump_e0 = (cells[4] - cells[3]) * (m[3] * m[4])
    jump_e1 = (cells[5] - cells[4]) * (m[4] * m[5])

    def pair(low, high):
        return jnp.where(even, low, turn(high, 1))

    odd_lon = lax.rem(lax.axis_index(lon_name), 2) == 1
    odd_lat = lax.rem(lax.axis_index(lat_name), 2) == 1
    east = (pair(cells[5], jump_e1), pair(d_cols[3], v_cols[2]), pair(s_cols[2], m[5]))
    west = (pair(cells[0], jump_01), d_cols[0], pair(zero, m[0]))
    for n in range(3):
        pay_c[n] = jnp.where(odd_lon, west[n], east[n])
        pay_d[n] = jnp.where(odd_lon, east[n], west[n])
    for n, x in enumerate(
        [cells[0], cells[1], jump_12, cells[4], cells[5], jump_e0] + d_cols + v_cols + s_cols
    ):
        own_lon[n] = x

    for b in range(items // ROWS):
        at = pl.ds(b * ROWS, ROWS)
        level = (sub + b * ROWS) // tracers
        m = [
            jnp.where(level < jnp.broadcast_to(x, (ROWS, cols)), 1.0, 0.0) for x in row_bottoms
        ]
        x = [y * z for y, z in zip(block[b], m)]
        j01 = (x[1] - x[0]) * (m[0] * m[1])
        j12 = (x[2] - x[1]) * (m[1] * m[2])
        k0 = (x[4] - x[3]) * (m[3] * m[4])
        k1 = (x[5] - x[4]) * (m[4] * m[5])
        for n, y in enumerate((x[0], x[1], j12, x[4], x[5], k0)):
            own_lat[n, at, :] = y
        pay_a[at, :] = jnp.where(odd_lat, x[0], x[5])
        pay_b[at, :] = jnp.where(odd_lat, x[5], x[0])
        at = pl.ds(items + b * ROWS, ROWS)
        pay_a[at, :] = jnp.where(odd_lat, j01, k1)
        pay_b[at, :] = jnp.where(odd_lat, k1, j01)
    base = 2 * items
    for k in range(levels):
        values = (
            diff_v[k, 0:1, :],
            diff_v[k, 1:2, :],
            diff_v[k, rows - 2 : rows - 1, :],
            diff_v[k, rows - 1 : rows, :],
            north_v[0, k, 0:1, :],
            north_v[1, k, 6:7, :],
            north_v[1, k, 7:8, :],
            north_v[2, k, 0:1, :],
            north_v[3, k, 6:7, :],
            north_v[3, k, 7:8, :],
        )
        for n, y in enumerate(values):
            own_lat_coef[n, k : k + 1, :] = y
        for n, top in enumerate((values[3], values[6], values[9])):
            low = values[0] if n == 0 else jnp.zeros_like(top)
            r = base + n * levels + k
            pay_a[r : r + 1, :] = jnp.where(odd_lat, low, top)
            pay_b[r : r + 1, :] = jnp.where(odd_lat, top, low)
    r = base + 3 * levels
    low, top = row_bottoms[0].astype(F32), row_bottoms[5].astype(F32)
    pay_a[r : r + 1, :] = jnp.where(odd_lat, low, top)
    pay_b[r : r + 1, :] = jnp.where(odd_lat, top, low)
    for q in range(r + 1, pay_a.shape[0]):
        pay_a[q : q + 1, :] = jnp.zeros_like(low)
        pay_b[q : q + 1, :] = jnp.zeros_like(low)


def pack(tracer, east_vel, north_vel, diff, east_slope, north_slope, bottom):
    tracers, levels, rows, cols = tracer.shape
    items = tracers * levels
    lat_rows = -(-(2 * items + 3 * levels + 1) // ROWS) * ROWS
    shape = jax.ShapeDtypeStruct
    vmem = pl.BlockSpec(memory_space=pltpu.VMEM)

    def body(*refs):
        pack_kernel(levels, tracers, rows, cols, "lon", "lat", *refs)

    return pl.pallas_call(
        body,
        name="pack_edges",
        in_specs=[pl.BlockSpec(memory_space=pltpu.HBM)] * 7,
        out_specs=[vmem] * 7,
        out_shape=[
            shape((lat_rows, cols), F32),
            shape((lat_rows, cols), F32),
            shape((3, rows, LANES), F32),
            shape((3, rows, LANES), F32),
            shape((16, rows, LANES), F32),
            shape((6, items, cols), F32),
            shape((10, levels, cols), F32),
        ],
        scratch_shapes=[
            pltpu.VMEM((tracers, levels, rows, cols), F32),
            pltpu.VMEM((levels, rows, cols), F32),
            pltpu.VMEM((levels, rows, cols), F32),
            pltpu.VMEM((levels, rows, cols), F32),
            pltpu.VMEM((4, levels, ROWS, cols), F32),
            pltpu.VMEM((rows, cols), jnp.int32),
            pltpu.SemaphoreType.DMA((levels // 3, 4)),
            pltpu.SemaphoreType.DMA((5,)),
        ],
        compiler_params=pltpu.CompilerParams(vmem_limit_bytes=VMEM_LIMIT),
        cost_estimate=pl.CostEstimate(flops=10**6, bytes_accessed=7 * 10**6, transcendentals=0),
    )(tracer, east_vel, north_vel, diff, east_slope, north_slope, bottom)


def interior_kernel(levels, tracers, rows, cols, span, *refs):
    sources = refs[:6]
    bottom_hbm, explicit_hbm = refs[6], refs[-23]
    (
        tracer,
        east_vel,
        north_vel,
        diff,
        east_slope,
        north_slope,
        bottom,
        explicit,
        sems,
        bottom_sem,
        out_sems,
        ring,
        ring_sum,
        step_here,
        step_west,
        bend_here,
        bend_east,
        flux_west,
        partial,
        north_part,
        open_at,
        coef,
    ) = refs[-22:]
    first, stop = span()
    blocks = rows // ROWS
    halves = (slice(0, LANES), slice(LANES, 2 * LANES))
    lane = iota((ROWS, LANES), 1)
    sub = iota((ROWS, LANES), 0)

    def chunk(b):
        return slice(b * ROWS, (b + 1) * ROWS)

    def east_of(x):
        left, right = x
        turned = pltpu.roll(right, LANES - 1, axis=1)
        return (
            jnp.where(lane == LANES - 1, turned, pltpu.roll(left, LANES - 1, axis=1)),
            turned,
        )

    def west_of(x):
        left, right = x
        turned = pltpu.roll(left, 1, axis=1)
        return turned, jnp.where(lane == 0, turned, pltpu.roll(right, 1, axis=1))

    def up(x):
        return tuple(pltpu.roll(y, ROWS - 1, axis=0) for y in x)

    def down(x):
        return tuple(pltpu.roll(y, 1, axis=0) for y in x)

    def north_of(turned, turned_next):
        if turned_next is None:
            return turned
        return tuple(jnp.where(sub == ROWS - 1, n, y) for y, n in zip(turned, turned_next))

    def south_of(turned, turned_before):
        if turned_before is None:
            return turned
        return tuple(jnp.where(sub == 0, n, y) for y, n in zip(turned, turned_before))

    def load(ref, *index):
        *lead, b = index
        return tuple(ref[(*lead, chunk(b), h)] for h in halves)

    def save(ref, values, *index):
        *lead, b = index
        for h, x in zip(halves, values):
            ref[(*lead, chunk(b), h)] = x

    def sub2(x, y):
        return tuple(p - q for p, q in zip(x, y))

    def add2(x, y):
        return tuple(p + q for p, q in zip(x, y))

    def low2(x, y):
        return tuple(jnp.minimum(p, q) for p, q in zip(x, y))

    units = [(t, b) for b in range(blocks) for t in range(tracers)]

    def fetch(n, level):
        src, dst = sources[n], (tracer, east_vel, north_vel, diff, east_slope, north_slope)[n]
        if n == 0:
            src, dst = src.at[:, level], dst.at[:, level]
        else:
            src, dst = src.at[level], dst.at[level]
        return pltpu.make_async_copy(src, dst, sems.at[n, level])

    def store(level):
        return pltpu.make_async_copy(
            explicit.at[:, level], explicit_hbm.at[:, level], out_sems.at[level]
        )

    def each_level(low, high, body):
        def run(level, carry):
            body(level)
            return carry

        lax.fori_loop(low, high, run, 0)

    def take_in(level, slot, out):
        at = jnp.clip(level, 0, levels - 1)
        depth = jnp.where(level < 0, levels, level)
        for b in range(blocks):
            sea = tuple(x > depth for x in load(bottom, b))
            for t in range(tracers):
                here = tuple(
                    jnp.where(s, x, 0.0) for s, x in zip(sea, load(tracer, t, at, b))
                )
                east = east_of(here)
                save(ring, here, slot, t, b)
                save(ring_sum, add2(here, east), slot, t, b)
                save(step_here, sub2(east, here), out, t, b)

    def take_steps(out):
        for t, b in units:
            save(step_west, west_of(load(step_here, out, t, b)), out, t, b)

    before_first = jnp.maximum(first - 1, 0)
    past_last = jnp.minimum(stop + 1, levels)
    started = first < stop

    @pl.when(started)
    def _():
        at_bottom = pltpu.make_async_copy(bottom_hbm, bottom, bottom_sem)
        at_bottom.start()

        def begin(level):
            fetch(0, level).start()

            @pl.when((level >= first) & (level < stop))
            def _():
                for n in range(1, 6):
                    fetch(n, level).start()

        each_level(before_first, past_last, begin)
        at_bottom.wait()
        depth = [load(bottom, b) for b in range(blocks)]
        ups, downs = [up(x) for x in depth], [down(x) for x in depth]
        east = [low2(x, east_of(x)) for x in depth]
        east_both = [low2(x, west_of(x)) for x in east]
        north = [
            low2(x, north_of(ups[b], ups[b + 1] if b + 1 < blocks else None))
            for b, x in enumerate(depth)
        ]
        north_downs = [down(x) for x in north]
        north_both = [
            low2(x, south_of(north_downs[b], north_downs[b - 1] if b else None))
            for b, x in enumerate(north)
        ]
        north_ups = [up(x) for x in north_both]
        for b in range(blocks):
            row = sub + b * ROWS
            inner_rows = (row > 0) & (row < rows - 2)
            inner = tuple(
                (lane + i * LANES > 0) & (lane + i * LANES < cols - 2) for i in range(2)
            )
            save(open_at, tuple(jnp.where(c, x, 0) for c, x in zip(inner, east[b])), 0, b)
            save(open_at, east_both[b], 1, b)
            save(open_at, east_of(east_both[b]), 2, b)
            save(open_at, tuple(jnp.where(inner_rows, x, 0) for x in north[b]), 3, b)
            save(open_at, north_both[b], 4, b)
            save(
                open_at,
                north_of(north_ups[b], north_ups[b + 1] if b + 1 < blocks else None),
                5,
                b,
            )
        @pl.when(first > 0)
        def _():
            fetch(0, first - 1).wait()

        fetch(0, first).wait()
        take_in(first - 1, lax.rem(first + 2, 3), lax.rem(first + 1, 2))
        take_in(first, lax.rem(first, 3), lax.rem(first, 2))
        take_steps(lax.rem(first, 2))

    def one_level(level):
        now, later, before = lax.rem(level, 3), lax.rem(level + 1, 3), lax.rem(level + 2, 3)
        nth = lax.rem(level, 2)
        nth_next = 1 - nth
        for n in range(1, 6):
            fetch(n, level).wait()

        @pl.when(level + 1 < levels)
        def _():
            fetch(0, level + 1).wait()

        for t, b in units:
            bend = tuple(
                minmod(x, y)
                for x, y in zip(load(step_here, nth, t, b), load(step_west, nth, t, b))
            )
            save(bend_here, bend, t, b)
            save(bend_east, east_of(bend), t, b)

        take_in(level + 1, later, nth_next)

        for b in range(blocks):
            here = load(diff, level, b)
            north = north_of(up(here), up(load(diff, level, min(b + 1, blocks - 1))))
            for way, other, vel, slope in (
                (0, east_of(here), east_vel, east_slope),
                (1, north, north_vel, north_slope),
            ):
                for i, h in enumerate(halves):
                    at = (chunk(b), h)
                    face = open_at[(3 * way, *at)] > level
                    speed = jnp.where(face, vel[(level, *at)], 0.0)
                    mean = jnp.where(face, 0.5 * (here[i] + other[i]), 0.0)
                    depth = jnp.where(
                        speed >= 0, open_at[(3 * way + 1, *at)], open_at[(3 * way + 2, *at)]
                    )
                    coef[(4 * way, *at)] = speed
                    coef[(4 * way + 1, *at)] = jnp.where(depth > level, limiter_weight(speed), 0.0)
                    coef[(4 * way + 2, *at)] = mean - jnp.minimum(speed, 0.0)
                    coef[(4 * way + 3, *at)] = 0.125 * slope[(level, *at)] * mean

        def face(way, b, here, step, bend, bend_other, tilt):
            out = []
            for i, h in enumerate(halves):
                at = (chunk(b), h)
                speed = coef[(4 * way, *at)]
                limited = jnp.where(speed >= 0, bend[i], bend_other[i])
                out.append(
                    (coef[(4 * way + 2, *at)] * step[i] - coef[(4 * way + 3, *at)] * tilt[i])
                    - (speed * here[i] + coef[(4 * way + 1, *at)] * limited)
                )
            return tuple(out)

        def north_faces(t):
            def stage(b):
                here = load(ring, now, t, b)
                tilt = sub2(load(ring, later, t, b), load(ring, before, t, b))
                return here, up(here), tilt, up(tilt)

            this = stage(0)
            step_before = flux_before = held = None
            for b in range(blocks + 1):
                if b < blocks:
                    nxt = stage(b + 1) if b + 1 < blocks else (None,) * 4
                    here, turned, tilt, tilt_turned = this
                    north = north_of(turned, nxt[1])
                    step = sub2(north, here)
                    step_turned = down(step)
                    bend = tuple(
                        minmod(x, y) for x, y in zip(step, south_of(step_turned, step_before))
                    )
                    bend_turned = up(bend)
                    step_before = step_turned
                if held is not None:
                    pb, p_here, p_step, p_bend, p_bend_turned, p_tilt = held
                    bend_n = north_of(p_bend_turned, bend_turned if b < blocks else None)
                    flux = face(1, pb, p_here, p_step, p_bend, bend_n, p_tilt)
                    flux_turned = down(flux)
                    if flux_before is None:
                        flux_s = tuple(jnp.where(sub == 0, 0.0, y) for y in flux_turned)
                    else:
                        flux_s = south_of(flux_turned, flux_before)
                    flux_before = flux_turned
                    save(north_part, add2(p_here, sub2(flux, flux_s)), t, pb)
                if b < blocks:
                    held = (
                        b, here, step, bend, bend_turned,
                        add2(tilt, north_of(tilt_turned, nxt[3])),
                    )
                    this = nxt

        for t in range(0, tracers, 2):
            north_faces(t)

        for t, b in units:
            flux = face(
                0,
                b,
                load(ring, now, t, b),
                load(step_here, nth, t, b),
                load(bend_here, t, b),
                load(bend_east, t, b),
                sub2(load(ring_sum, later, t, b), load(ring_sum, before, t, b)),
            )
            left, right = west_of(flux)
            save(flux_west, (jnp.where(lane == 0, 0.0, left), right), t, b)
            save(partial, flux, t, b)

        take_steps(nth_next)

        for t in range(1, tracers, 2):
            north_faces(t)

        for t, b in units:
            total = add2(
                load(north_part, t, b), sub2(load(partial, t, b), load(flux_west, t, b))
            )
            save(explicit, total, t, level, b)

        store(level).start()

    each_level(first, stop, one_level)
    each_level(first, stop, lambda level: store(level).wait())


def interior(tracer, east_vel, north_vel, diff, east_slope, north_slope, bottom, span, so_far=None):
    tracers, levels, rows, cols = tracer.shape

    def body(*refs):
        interior_kernel(levels, tracers, rows, cols, span, *refs)

    plane = (tracers, rows, cols)
    field = pltpu.VMEM((levels, rows, cols), F32)
    args = (tracer, east_vel, north_vel, diff, east_slope, north_slope, bottom)
    args = args if so_far is None else (*args, so_far)
    hbm = pl.BlockSpec(memory_space=pltpu.HBM)
    return pl.pallas_call(
        body,
        name="interior_faces",
        in_specs=[hbm] * len(args),
        out_specs=hbm,
        out_shape=jax.ShapeDtypeStruct(tracer.shape, F32),
        input_output_aliases={} if so_far is None else {7: 0},
        scratch_shapes=[
            pltpu.VMEM(tracer.shape, F32),
            field,
            field,
            field,
            field,
            field,
            pltpu.VMEM((rows, cols), jnp.int32),
            pltpu.VMEM(tracer.shape, F32),
            pltpu.SemaphoreType.DMA((6, levels)),
            pltpu.SemaphoreType.DMA,
            pltpu.SemaphoreType.DMA((levels,)),
            pltpu.VMEM((3, *plane), F32),
            pltpu.VMEM((3, *plane), F32),
            pltpu.VMEM((2, *plane), F32),
            pltpu.VMEM((2, *plane), F32),
            pltpu.VMEM(plane, F32),
            pltpu.VMEM(plane, F32),
            pltpu.VMEM(plane, F32),
            pltpu.VMEM(plane, F32),
            pltpu.VMEM(plane, F32),
            pltpu.VMEM((6, rows, cols), jnp.int32),
            pltpu.VMEM((8, rows, cols), F32),
        ],
        compiler_params=pltpu.CompilerParams(vmem_limit_bytes=VMEM_LIMIT),
        cost_estimate=pl.CostEstimate(
            flops=60 * tracer.size, bytes_accessed=12 * 10**6, transcendentals=0
        ),
    )(*args)


def edge_faces(m1, m2, m3, j0, j3, open1, open2, d1, d2, d3, v0, v1, s0, s1, tilt):
    j1 = (m2 - m1) * open1
    j2 = (m3 - m2) * open2
    t1, t2, t3 = tilt(m1), tilt(m2), tilt(m3)

    def face(low, high, behind, jump, ahead, opened, d_sum, vel, slope, tilts):
        speed = vel * opened
        forward = speed >= 0
        flux = speed * jnp.where(forward, low, high) + limiter_weight(speed) * minmod(
            jump, jnp.where(forward, behind, ahead)
        )
        return 0.5 * d_sum * (jump - 0.125 * slope * opened * tilts) - flux

    return (
        face(m1, m2, j0, j1, j2, open1, d1 + d2, v0, s0, t1 + t2),
        face(m2, m3, j1, j2, j3, open2, d2 + d3, v1, s1, t2 + t3),
    )


def solve_kernel(levels, tracers, rows, cols, lon_name, lat_name, lat_count, *refs):
    (
        explicit_hbm,
        vertical_hbm,
        bottom,
        got_a,
        got_b,
        got_c,
        got_d,
        own_lon,
        own_lat,
        own_lat_coef,
        out_hbm,
        field,
        vertical,
        fix_lon,
        fix_lat,
        south,
        north,
        pivots,
        in_sems,
        out_sems,
    ) = refs
    blocks = rows // ROWS
    items = levels * tracers
    base = 2 * items
    halves = (slice(0, LANES), slice(LANES, 2 * LANES))
    lane = iota((ROWS, LANES), 1)
    sub = iota((ROWS, LANES), 0)

    def rows_of(b):
        if isinstance(b, int):
            return pl.ds(b * ROWS, ROWS)
        return pl.ds(pl.multiple_of(b * ROWS, ROWS), ROWS)

    def fetch(b):
        at = rows_of(b)
        return (
            pltpu.make_async_copy(
                explicit_hbm.at[:, :, at, :], field.at[:, :, at, :], in_sems.at[0, b]
            ),
            pltpu.make_async_copy(
                vertical_hbm.at[:, at, :], vertical.at[:, at, :], in_sems.at[1, b]
            ),
        )

    def store(b):
        at = rows_of(b)
        return pltpu.make_async_copy(
            field.at[:, :, at, :], out_hbm.at[:, :, at, :], out_sems.at[b]
        )

    for b in range(blocks):
        for copy in fetch(b):
            copy.start()

    def edges():
        odd_lon = lax.rem(lax.axis_index(lon_name), 2) == 1
        lat = lax.axis_index(lat_name)
        odd_lat = lax.rem(lat, 2) == 1
        top = lat == lat_count - 1
        even = lane % 2 == 0
        inside = lane < 2 * items
        level = lane // (2 * tracers)

        def tilt_lanes(x):
            return pltpu.roll(x, LANES - 2 * tracers, axis=1) - pltpu.roll(
                x, 2 * tracers, axis=1
            )

        for b in range(blocks):
            at = slice(b * ROWS, (b + 1) * ROWS)

            def mask(c):
                col = jnp.broadcast_to(bottom[at, c : c + 1], (ROWS, LANES))
                return jnp.where((level < col) & inside, 1.0, 0.0)

            def halves_of(pays):
                return pays, [pltpu.roll(x, LANES - 1, axis=1) for x in pays]

            c_got = [got_c[n, at, :] for n in range(3)]
            d_got = [got_d[n, at, :] for n in range(3)]
            from_west = [jnp.where(odd_lon, c, d) for c, d in zip(c_got, d_got)]
            from_east = [jnp.where(odd_lon, d, c) for c, d in zip(c_got, d_got)]
            own = [own_lon[n, at, :] for n in range(16)]
            (wm, wd, ws), (wj, wv, wk) = halves_of(from_west)
            m0, m1 = mask(0), mask(1)
            f0, f1 = edge_faces(
                wm, own[0], own[1], wj, own[2], wk * m0, m0 * m1,
                wd, own[6], own[7], wv, own[10], ws, own[13], tilt_lanes,
            )
            fix_lon[0, at, :] = jnp.where(
                even, (f1 - f0) * m0, pltpu.roll(-f1 * m1, 1, axis=1)
            )
            (em, ed, _), (ej, _, ek) = halves_of(from_east)
            m0, m1 = mask(cols - 2), mask(cols - 1)
            f0, f1 = edge_faces(
                own[3], own[4], em, own[5], ej, m0 * m1, m1 * ek,
                own[8], own[9], ed, own[11], own[12], own[14], own[15], tilt_lanes,
            )
            fix_lon[1, at, :] = jnp.where(
                even, f0 * m0, pltpu.roll((f1 - f0) * m1, 1, axis=1)
            )

        south[...] = jnp.where(odd_lat, got_a[...], got_b[...])

        @pl.when(jnp.logical_not(top))
        def _():
            north[...] = jnp.where(odd_lat, got_b[...], got_a[...])

        @pl.when(top)
        def _():
            mirror = LANES - 1 - lane
            for b in range(north.shape[0] // ROWS):
                at = slice(b * ROWS, (b + 1) * ROWS)
                for i in range(2):
                    north[at, halves[i]] = jnp.take_along_axis(
                        got_b[at, halves[1 - i]], mirror, axis=1, mode="promise_in_bounds"
                    )

        wide = iota((ROWS, cols), 0)
        sign = jnp.where(top, -1.0, 1.0)

        def spread_rows(ref, first, b):
            k = b * ROWS // tracers
            low, high = ref[first + k : first + k + 1, :], ref[first + k + 1 : first + k + 2, :]
            return jnp.where(
                wide < tracers,
                jnp.broadcast_to(low, (ROWS, cols)),
                jnp.broadcast_to(high, (ROWS, cols)),
            )

        def tilt_rows_of(read):
            def tilt(b):
                here = read(b)
                zeros = jnp.zeros_like(here)
                turned = pltpu.roll(here, tracers, axis=0)
                after = pltpu.roll(read(b + 1), tracers, axis=0) if b + 1 < items // ROWS else zeros
                before = pltpu.roll(read(b - 1), tracers, axis=0) if b else zeros
                return jnp.where(wide < tracers, turned, after) - jnp.where(
                    wide < tracers, before, turned
                )

            return tilt

        def own_row(n):
            return lambda b: own_lat[n, b * ROWS : (b + 1) * ROWS, :]

        def ghost_row(ref):
            return lambda b: ref[b * ROWS : (b + 1) * ROWS, :]

        for b in range(items // ROWS):
            at = slice(b * ROWS, (b + 1) * ROWS)
            past = slice(items + b * ROWS, items + (b + 1) * ROWS)
            level = (wide + b * ROWS) // tracers

            def mask(row):
                return jnp.where(level < jnp.broadcast_to(row, (ROWS, cols)), 1.0, 0.0)

            def coef(n):
                return spread_rows(own_lat_coef.at[n], 0, b)

            def ghost_mask(ref):
                row = ref[base + 3 * levels : base + 3 * levels + 1, :]
                return jnp.where(level.astype(F32) < jnp.broadcast_to(row, (ROWS, cols)), 1.0, 0.0)

            south_mask = jnp.where(lat > 0, ghost_mask(south), 0.0)

            def run(reads, j0, j3, open1, open2, d, v, s):
                tilts = [tilt_rows_of(r)(b) for r in reads]
                values = [r(b) for r in reads]
                lookup = dict(zip(map(id, values), tilts))
                return edge_faces(*values, j0, j3, open1, open2, *d, *v, *s,
                                  lambda x: lookup[id(x)])

            m0, m1 = mask(bottom[0:1, :]), mask(bottom[1:2, :])
            f0, f1 = run(
                (ghost_row(south), own_row(0), own_row(1)),
                jnp.where(lat > 0, south[past, :], 0.0), own_lat[2, at, :], south_mask * m0, m0 * m1,
                (spread_rows(south, base, b), coef(0), coef(1)),
                (spread_rows(south, base + levels, b), coef(4)),
                (spread_rows(south, base + 2 * levels, b), coef(7)),
            )
            fix_lat[0, at, :] = (f1 - f0) * m0
            fix_lat[1, at, :] = -f1 * m1
            m0 = mask(bottom[rows - 2 : rows - 1, :])
            m1 = mask(bottom[rows - 1 : rows, :])
            top_vel = coef(6)
            ghost_vel = spread_rows(north, base + levels, b)
            top_vel = jnp.where(top, 0.5 * (top_vel - ghost_vel), top_vel)
            f0, f1 = run(
                (own_row(3), own_row(4), ghost_row(north)),
                own_lat[5, at, :], sign * north[past, :], m0 * m1, m1 * ghost_mask(north),
                (coef(2), coef(3), spread_rows(north, base, b)),
                (coef(5), top_vel),
                (coef(8), coef(9)),
            )
            fix_lat[2, at, :] = f0 * m0
            fix_lat[3, at, :] = (f1 - f0) * m1

    edges()

    def one_block(step, carry):
        at = rows_of(step)
        for copy in fetch(step):
            copy.wait()
        first_block = step == 0
        row0 = jnp.where(first_block, 0, ROWS - 2)
        pick = jnp.where(first_block, 0, 2)

        @pl.when(first_block | (step == blocks - 1))
        def _():
            for t in range(tracers):
                for k in range(levels):
                    n = k * tracers + t
                    for h in halves:
                        low = jnp.broadcast_to(fix_lat[pick, n : n + 1, h], (ROWS, LANES))
                        high = jnp.broadcast_to(fix_lat[pick + 1, n : n + 1, h], (ROWS, LANES))
                        field[t, k, at, h] = field[t, k, at, h] + jnp.where(
                            sub == row0, low, jnp.where(sub == row0 + 1, high, 0.0)
                        )

        depth = tuple(bottom[at, h] for h in halves)
        for i, h in enumerate(halves):
            ratio = above = None
            for k in range(levels):
                if k + 1 < levels:
                    below = jnp.where(depth[i] > k + 1, vertical[k, at, h], 0.0)
                if k == 0:
                    pivot = 1.0 + below
                elif k + 1 < levels:
                    pivot = (1.0 + above + below) + above * ratio
                else:
                    pivot = (1.0 + above) + above * ratio
                inverse = 1.0 / pivot
                pivots[0, k, :, h] = inverse
                if k:
                    pivots[1, k, :, h] = above
                if k + 1 < levels:
                    ratio = below * inverse
                    pivots[2, k, :, h] = ratio
                    above = below

        fixes = [fix_lon[i, at, :] for i in range(2)]
        for t in range(tracers):
            for i, h in enumerate(halves):
                begin = 0 if i == 0 else LANES - 2
                near = lane < 2 if i == 0 else lane >= LANES - 2
                values = []
                value = None
                for k in range(levels):
                    turn = (begin - 2 * (k * tracers + t)) % LANES
                    patch = pltpu.roll(fixes[i], turn, axis=1) if turn else fixes[i]
                    right = field[t, k, at, h] + jnp.where(near, patch, 0.0)
                    right = jnp.where(depth[i] > k, right, 0.0)
                    if k:
                        right = right + pivots[1, k, :, h] * value
                    value = right * pivots[0, k, :, h]
                    values.append(value)
                nxt = values[-1]
                field[t, levels - 1, at, h] = nxt
                for k in range(levels - 2, -1, -1):
                    nxt = values[k] + pivots[2, k, :, h] * nxt
                    field[t, k, at, h] = nxt
        store(step).start()
        return carry

    lax.fori_loop(0, blocks, one_block, 0)
    for b in range(blocks):
        store(b).wait()


def solve(explicit, vertical, bottom, got, own):
    tracers, levels, rows, cols = explicit.shape
    items = levels * tracers
    lat_rows = got[0].shape[0]
    lat_count = lax.axis_size("lat")
    blocks = rows // ROWS

    def body(*refs):
        solve_kernel(levels, tracers, rows, cols, "lon", "lat", lat_count, *refs)

    hbm = pl.BlockSpec(memory_space=pltpu.HBM)
    vmem = pl.BlockSpec(memory_space=pltpu.VMEM)
    return pl.pallas_call(
        body,
        name="edges_and_solve",
        in_specs=[hbm, hbm] + [vmem] * 8,
        out_specs=hbm,
        out_shape=jax.ShapeDtypeStruct(explicit.shape, F32),
        input_output_aliases={0: 0},
        scratch_shapes=[
            pltpu.VMEM(explicit.shape, F32),
            pltpu.VMEM(vertical.shape, F32),
            pltpu.VMEM((2, rows, LANES), F32),
            pltpu.VMEM((4, items, cols), F32),
            pltpu.VMEM((lat_rows, cols), F32),
            pltpu.VMEM((lat_rows, cols), F32),
            pltpu.VMEM((3, levels, ROWS, cols), F32),
            pltpu.SemaphoreType.DMA((2, blocks)),
            pltpu.SemaphoreType.DMA((blocks,)),
        ],
        compiler_params=pltpu.CompilerParams(vmem_limit_bytes=SOLVE_LIMIT),
        cost_estimate=pl.CostEstimate(
            flops=20 * explicit.size, bytes_accessed=8 * 10**6, transcendentals=0
        ),
    )(explicit, vertical, bottom, *got, *own)


def local(
    tracer,
    east_velocity,
    north_velocity,
    diffusivity,
    east_slope,
    north_slope,
    vertical_diffusivity,
    sea_mask,
    bottom,
):
    lon, lat = lax.axis_size("lon"), lax.axis_size("lat")
    levels = tracer.shape[1]
    args = (tracer, east_velocity, north_velocity, diffusivity, east_slope, north_slope, bottom)
    pay_a, pay_b, pay_c, pay_d, *own = pack(*args)

    def swap(pairs):
        return [p for a, b in pairs for p in ((a, b), (b, a))]

    def at(i, j):
        return i * lat + j

    near_lat = swap([(j, j + 1) for j in range(0, lat, 2)])
    far_lat = swap([(at(i, j), at(i, j + 1)) for i in range(lon) for j in range(1, lat - 1, 2)])
    far_lat += [(at(i, lat - 1), at(lon - 1 - i, lat - 1)) for i in range(lon)]
    far_lat += swap([(at(i, 0), at(i + 1, 0)) for i in range(0, lon, 2)])
    near_lon = swap([(i, i + 1) for i in range(0, lon, 2)])
    far_lon = swap([(i, (i + 1) % lon) for i in range(1, lon, 2)])
    got_a = lax.ppermute(pay_a, "lat", near_lat)
    got_c = lax.ppermute(pay_c, "lon", near_lon)
    got_b = lax.ppermute(pay_b, ("lon", "lat"), far_lat)
    got_d = lax.ppermute(pay_d, "lon", far_lon)
    explicit = interior(*args, lambda: (0, levels))
    return solve(
        explicit, vertical_diffusivity, bottom, (got_a, got_b, got_c, got_d), tuple(own)
    )


def solution(mesh):
    field = P(None, "lat", "lon")
    placed = (
        P(None, None, "lat", "lon"),
        field,
        field,
        field,
        field,
        field,
        field,
        field,
        P("lat", "lon"),
    )
    return jax.shard_map(
        local, mesh=mesh, in_specs=placed, out_specs=P(None, None, "lat", "lon"), check_vma=False
    )
```

time: 50.9 us -> 31.7 us (0.62)
  Pallas kernels: 29.4 us -> 20.8 us
  local copies, waits for them, and re-layouts: 8.4 us -> 0.02 us
  starting transfers between devices: 12.6 us -> 10.6 us
    pallas_call x2, Pallas kernels: 23 us -> 14.3 us  [the longest x1 10.4 us: interior(): pl.pallas_call(body, name='interior_faces', in_specs=[hbm] * len(args), o...]
    unnamed x18 -> x10, local copies, waits for them, and re-layouts: 8.4 us -> 0.02 us
    ppermute x1, starting transfers between devices: 4.96 us -> 3.06 us  [local(): got_b = lax.ppermute(pay_b, ('lon', 'lat'), far_lat)]
  transfers between devices with their start and end apart: 4 -> 4, of which waited for: 0 -> 0; matrix products, arithmetic and copies ran while one was open for 0% -> 0% of each run, Pallas kernels for 34% -> 33%
where the time goes in v1:
time: 31.7 us; the launch traced here: 31.6 us
  Pallas kernels  20.8 us (66%)
  starting transfers between devices  10.6 us (33%)
    pallas_call x1, Pallas kernels, interior(): pl.pallas_call(body, name='interior_faces', in_specs=[hbm] * len(args), o...  10.4 us
    pallas_call x1, Pallas kernels, pack(): pl.pallas_call(body, name='pack_edges', in_specs=[pl.BlockSpec(memory_spa...  6.54 us
    ppermute x1, starting transfers between devices, local(): got_d = lax.ppermute(pay_d, 'lon', far_lon)  5.39 us
    pallas_call x1, Pallas kernels, solve(): pl.pallas_call(body, name='edges_and_solve', in_specs=[hbm, hbm] + [vmem]...  3.88 us
    ppermute x1, starting transfers between devices, local(): got_b = lax.ppermute(pay_b, ('lon', 'lat'), far_lat)  3.06 us
    ppermute x1, starting transfers between devices, local(): got_c = lax.ppermute(pay_c, 'lon', near_lon)  2.1 us
  transfers between devices with their start and end apart: 4, of which 0 were waited for; matrix products, arithmetic and copies ran while one was open for 0% of the time, Pallas kernels for 33%

profile of v1, /device:TPU:4, one launch (start us, length us, event | category | flops | bytes accessed | tf_op | source)
XLA Modules:
  0.0 31.6 jit_solution(17284990294135058851)
XLA Ops:
  0.0 6.5 %pack_edges.1 = (f32[136,256]{1,0:T(8,128)}, f32[136,256]{1,0:T(8,128)}, f32[3,64,128]{2,1,0:T(8,128)}, f32[3,64,128]{2,1,0:T(8,128)}, f32[16,64,128]{2,1,0:T(8,...) custom-call(f32[4,12,64,256]{3,2,1,0:T(8,128)} %refs_0_.3, f32[12,64,256]{2,1,0:T(8,128)} %refs_1_.4, ...), custom_call_target="tpu_custom_call" | custom-call | flops 1000000 | bytes 7000000 | tf_op jit(solution)/shard_map/pack_edges/pallas_call | solution.py:237
  6.5 0.1 collective-permute-start
  6.6 3.1 %collective-permute-start.1 = (f32[136,256]{1,0:T(8,128)}, f32[136,256]{1,0:T(8,128)S(1)}, u32[]{:S(2)}, u32[]{:S(2)}) collective-permute-start(f32[136,256]{1,0:T(8,128)} %get-tuple-element.13), channel_id=1, source_target_pairs={{1,2},{2,1},{3,4},{4,3},{5,6},{6,5},{7,8},{8,7},{9,10},{10,9},{11,... | collective-permute-start | bytes 417800 | tf_op jit(solution)/shard_map/ppermute | solution.py:980
  9.7 2.1 %collective-permute-start.2 = (f32[3,64,128]{2,1,0:T(8,128)}, f32[3,64,128]{2,1,0:T(8,128)S(1)}, u32[]{:S(2)}, u32[]{:S(2)}) collective-permute-start(f32[3,64,128]{2,1,0:T(8,128)} %get-tuple-element.14), channel_id=1, source_target_pairs={{0,16},{16,0},{32,48},{48,32},{64,80},{80,64},{96,112},{112,96},{1... | collective-permute-start | bytes 294920 | tf_op jit(solution)/shard_map/ppermute | solution.py:979
  11.8 0.0 copy-start
  11.8 0.0 copy-start.1
  11.8 0.0 copy-start.2
  11.8 0.0 copy-start.3
  11.8 0.0 copy-start.4
  11.8 5.4 %collective-permute-start.3 = (f32[3,64,128]{2,1,0:T(8,128)}, f32[3,64,128]{2,1,0:T(8,128)S(1)}, u32[]{:S(2)}, u32[]{:S(2)}) collective-permute-start(f32[3,64,128]{2,1,0:T(8,128)} %get-tuple-element.15), channel_id=1, source_target_pairs={{16,32},{32,16},{48,64},{64,48},{80,96},{96,80},{112,128},{128,112... | collective-permute-start | bytes 294920 | tf_op jit(solution)/shard_map/ppermute | solution.py:981
  17.2 10.4 %interior_faces.1.refs_0_ = f32[4,12,64,256]{3,2,1,0:T(8,128)} custom-call(f32[4,12,64,256]{3,2,1,0:T(8,128)} %refs_0_.3, f32[12,64,256]{2,1,0:T(8,128)} %refs_1_.4, f32[12,64,256]{2,1,0:T(8,128)} %refs_2_.4, f32[12,64,256]{2,1,0:T(8,128)} %refs_3_.3, f32[12,64,256]{2,1,0:T(8,128)} %refs_4_.3, f32[12,64,256]{2,1,0:T(8,128)} %refs_5_.3, s32[64,256]{1,0:T(8,128)} %refs_2_.5), custom_call_target="tpu_custom_call" | custom-call | flops 47185920 | bytes 12000000 | tf_op jit(solution)/shard_map/interior_faces/pallas_call | solution.py:584
  27.6 0.0 collective-permute-done.2.refs_5_
  27.7 0.0 collective-permute-done.3.refs_6_
  27.7 0.0 collective-permute-done.refs_3_
  27.7 0.0 collective-permute-done.1.refs_4_
  27.7 0.0 copy-done
  27.7 0.0 copy-done.1
  27.7 0.0 copy-done.2
  27.7 0.0 copy-done.3
  27.7 0.0 copy-done.4
  27.7 3.9 %edges_and_solve.1 = f32[4,12,64,256]{3,2,1,0:T(8,128)} custom-call(f32[4,12,64,256]{3,2,1,0:T(8,128)} %interior_faces.1.refs_0_, f32[11,64,256]{2,1,0:T(8,128)S(1)} %copy-done, s32[64,256]{1,0:T(8,128)S(1)} %copy-done.1, f32[136,256]{1,0:T(8,128)S(1)} %collective-permute-done.refs_3_, ...), custom_call_target="tpu_custom_call", output_to_operand_aliasing={{}: (0, {})} | custom-call | flops 15728640 | bytes 8000000 | tf_op jit(solution)/shard_map/edges_and_solve/pallas_call | solution.py:925
Async XLA Ops:
  6.5 21.1 %collective-permute-start = (f32[136,256]{1,0:T(8,128)}, f32[136,256]{1,0:T(8,128)S(1)}, u32[]{:S(2)}, u32[]{:S(2)}) collective-permute-start(f32[136,256]{1,0:T(8,128)} %get-tuple-element.12), channel_id=1, source_target_pairs={{0,1},{1,0},{2,3},{3,2},{4,5},{5,4},{6,7},{7,6},{8,9},{9,8},{10,11... | collective-permute-start | bytes 417800 | tf_op jit(solution)/shard_map/ppermute | solution.py:978
  6.6 21.0 %collective-permute-start.1 = (f32[136,256]{1,0:T(8,128)}, f32[136,256]{1,0:T(8,128)S(1)}, u32[]{:S(2)}, u32[]{:S(2)}) collective-permute-start(f32[136,256]{1,0:T(8,128)} %get-tuple-element.13), channel_id=1, source_target_pairs={{1,2},{2,1},{3,4},{4,3},{5,6},{6,5},{7,8},{8,7},{9,10},{10,9},{11,... | collective-permute-start | bytes 417800 | tf_op jit(solution)/shard_map/ppermute | solution.py:980
  9.7 17.9 %collective-permute-start.2 = (f32[3,64,128]{2,1,0:T(8,128)}, f32[3,64,128]{2,1,0:T(8,128)S(1)}, u32[]{:S(2)}, u32[]{:S(2)}) collective-permute-start(f32[3,64,128]{2,1,0:T(8,128)} %get-tuple-element.14), channel_id=1, source_target_pairs={{0,16},{16,0},{32,48},{48,32},{64,80},{80,64},{96,112},{112,96},{1... | collective-permute-start | bytes 294920 | tf_op jit(solution)/shard_map/ppermute | solution.py:979
  11.8 15.9 %copy-start = (f32[11,64,256]{2,1,0:T(8,128)S(1)}, f32[11,64,256]{2,1,0:T(8,128)}, u32[]{:S(2)}) copy-start(f32[11,64,256]{2,1,0:T(8,128)} %refs_1_.5) | copy-start | bytes 2162692
  11.8 15.9 %copy-start.1 = (s32[64,256]{1,0:T(8,128)S(1)}, s32[64,256]{1,0:T(8,128)}, u32[]{:S(2)}) copy-start(s32[64,256]{1,0:T(8,128)} %refs_2_.5) | copy-start | bytes 196612
  11.8 15.9 %copy-start.2 = (f32[16,64,128]{2,1,0:T(8,128)S(1)}, f32[16,64,128]{2,1,0:T(8,128)}, u32[]{:S(2)}) copy-start(f32[16,64,128]{2,1,0:T(8,128)} %get-tuple-element.16.refs_7_) | copy-start | bytes 1572868
  11.8 15.9 %copy-start.3 = (f32[6,48,256]{2,1,0:T(8,128)S(1)}, f32[6,48,256]{2,1,0:T(8,128)}, u32[]{:S(2)}) copy-start(f32[6,48,256]{2,1,0:T(8,128)} %get-tuple-element.17.refs_8_) | copy-start | bytes 884740
  11.8 15.9 %copy-start.4 = (f32[10,12,256]{2,1,0:T(8,128)S(1)}, f32[10,12,256]{2,1,0:T(8,128)}, u32[]{:S(2)}) copy-start(f32[10,12,256]{2,1,0:T(8,128)} %get-tuple-element.18.refs_9_) | copy-start | bytes 368644
  11.8 15.8 %collective-permute-start.3 = (f32[3,64,128]{2,1,0:T(8,128)}, f32[3,64,128]{2,1,0:T(8,128)S(1)}, u32[]{:S(2)}, u32[]{:S(2)}) collective-permute-start(f32[3,64,128]{2,1,0:T(8,128)} %get-tuple-element.15), channel_id=1, source_target_pairs={{16,32},{32,16},{48,64},{64,48},{80,96},{96,80},{112,128},{128,112... | collective-permute-start | bytes 294920 | tf_op jit(solution)/shard_map/ppermute | solution.py:981

commit v2 on v1

--- a/solution.py
+++ b/solution.py
@@ -8,7 +8,7 @@
 F32 = jnp.float32
 LANES = 128
 ROWS = 8
-VMEM_LIMIT = 61 << 20
+VMEM_LIMIT = 40 << 20
 SOLVE_LIMIT = 32 << 20
 
 
@@ -28,14 +28,8 @@
 
 
 def pack_kernel(levels, tracers, rows, cols, lon_name, lat_name, *refs):
+    sources = refs[:7]
     (
-        tracer_hbm,
-        east_vel_hbm,
-        north_vel_hbm,
-        diff_hbm,
-        east_slope_hbm,
-        north_slope_hbm,
-        bottom_hbm,
         pay_a,
         pay_b,
         pay_c,
@@ -47,17 +41,21 @@
         east_vel_v,
         diff_v,
         east_slope_v,
+        bottom_v,
         north_v,
-        bottom_v,
+        gathered,
+        turned_v,
         sems,
         row_sems,
-    ) = refs
+    ) = refs[7:]
+    tracer_hbm, east_vel_hbm, north_vel_hbm, diff_hbm, east_slope_hbm, north_slope_hbm = sources[:6]
     items = levels * tracers
-    group = 3
+    group = ROWS // tracers
     groups = levels // group
     last = rows - ROWS
-    copies = []
-    row_copies = [pltpu.make_async_copy(bottom_hbm, bottom_v, row_sems.at[0])]
+    right = cols - LANES
+    base = 2 * items
+    row_copies = [pltpu.make_async_copy(sources[6], bottom_v, row_sems.at[0])]
     for n, (src, start) in enumerate(
         ((north_vel_hbm, 0), (north_vel_hbm, last), (north_slope_hbm, 0), (north_slope_hbm, last))
     ):
@@ -66,6 +64,7 @@
                 src.at[:, pl.ds(start, ROWS), :], north_v.at[n], row_sems.at[n + 1]
             )
         )
+    copies = []
     for g in range(groups):
         span = pl.ds(g * group, group)
         fetch = [
@@ -78,184 +77,206 @@
         ):
             fetch.append(pltpu.make_async_copy(src.at[span], dst.at[span], sems.at[g, n + 1]))
         copies.append(fetch)
+    row_copies[0].start()
     for copy in copies[0]:
         copy.start()
-    for copy in row_copies:
+    for copy in row_copies[1:]:
         copy.start()
     for fetch in copies[1:]:
         for copy in fetch:
             copy.start()
 
-    lane = iota((rows, LANES), 1)
+    lane = iota((ROWS, LANES), 1)
     couple = lane // 2
     even = lane % 2 == 0
     left_side = lane < 64
     sub = iota((ROWS, cols), 0)
-    right = cols - LANES
-    zero = jnp.zeros((rows, LANES), F32)
-    first_two = second = third_last = last_two = zero
-    coefs = [[zero, zero] for _ in range(3)]
     row_at = (0, 1, 2, rows - 3, rows - 2, rows - 1)
-    for copy in row_copies:
-        copy.wait()
-    row_bottoms = [bottom_v[r : r + 1, :] for r in row_at]
-    block = [[jnp.zeros((ROWS, cols), F32)] * 6 for _ in range(items // ROWS)]
-    edge_bottom = jnp.where(left_side, bottom_v[:, :LANES], bottom_v[:, right:])
+    odd_lon = lax.rem(lax.axis_index(lon_name), 2) == 1
+    odd_lat = lax.rem(lax.axis_index(lat_name), 2) == 1
+    chunks = [slice(r * ROWS, (r + 1) * ROWS) for r in range(rows // ROWS)]
 
     def turn(x, by):
         by = by % LANES
         return pltpu.roll(x, by, axis=1) if by else x
 
+    def send_rows(at, low, top):
+        pay_a[at, :] = jnp.where(odd_lat, low, top)
+        pay_b[at, :] = jnp.where(odd_lat, top, low)
+
+    row_copies[0].wait()
+    row_bottoms = [bottom_v[r : r + 1, :] for r in row_at]
     for g in range(groups):
         for copy in copies[g]:
             copy.wait()
         for k in range(g * group, (g + 1) * group):
-            sea = edge_bottom > k
-            for t in range(tracers):
-                n = k * tracers + t
-                both = jnp.where(
-                    left_side, tracer_v[t, k, :, :LANES], tracer_v[t, k, :, right:]
-                )
-                turned = turn(jnp.where(sea, both, 0.0), 2 * n)
-                first_two = jnp.where(couple == n, turned, first_two)
-                last_two = jnp.where(couple == (n - 1) % 64, turned, last_two)
-                second = jnp.where(lane == 2 * n + 2, turned, second)
-                third_last = jnp.where(lane == (2 * n - 3) % LANES, turned, third_last)
-                for c, r in enumerate(row_at):
-                    block[n // ROWS][c] = jnp.where(
-                        sub == n % ROWS,
-                        jnp.broadcast_to(tracer_v[t, k, r : r + 1, :], (ROWS, cols)),
-                        block[n // ROWS][c],
+            j = (k - g * group) * (tracers + 3)
+            for at in chunks:
+                sea = jnp.where(left_side, bottom_v[at, :LANES], bottom_v[at, right:]) > k
+                for t in range(tracers):
+                    both = jnp.where(
+                        left_side, tracer_v[t, k, at, :LANES], tracer_v[t, k, at, right:]
                     )
-            n = k * tracers
-            for ref, outs in zip((diff_v, east_vel_v, east_slope_v), coefs):
-                turned = turn(jnp.where(left_side, ref[k, :, :LANES], ref[k, :, right:]), 2 * n)
-                outs[0] = jnp.where(couple == n, turned, outs[0])
-                outs[1] = jnp.where(couple == (n - 1) % 64, turned, outs[1])
+                    turned_v[j + t, at, :] = turn(
+                        jnp.where(sea, both, 0.0), 2 * (k * tracers + t)
+                    )
+                for i, ref in enumerate((diff_v, east_vel_v, east_slope_v)):
+                    both = jnp.where(left_side, ref[k, at, :LANES], ref[k, at, right:])
+                    turned_v[j + tracers + i, at, :] = turn(both, 2 * k * tracers)
+        first = g * group
+        x = []
+        m = []
+        level = sub // tracers + first
+        for c, r in enumerate(row_at):
+            rows_in = jnp.broadcast_to(tracer_v[0, first, r : r + 1, :], (ROWS, cols))
+            for q in range(1, ROWS):
+                row = tracer_v[q % tracers, first + q // tracers, r : r + 1, :]
+                rows_in = jnp.where(sub == q, jnp.broadcast_to(row, (ROWS, cols)), rows_in)
+            m.append(
+                jnp.where(level < jnp.broadcast_to(row_bottoms[c], (ROWS, cols)), 1.0, 0.0)
+            )
+            x.append(rows_in * m[c])
+        at = pl.ds(g * ROWS, ROWS)
+        for n, y in enumerate(
+            (
+                x[0],
+                x[1],
+                (x[2] - x[1]) * (m[1] * m[2]),
+                x[4],
+                x[5],
+                (x[4] - x[3]) * (m[3] * m[4]),
+            )
+        ):
+            own_lat[n, at, :] = y
+        send_rows(at, x[0], x[5])
+        send_rows(
+            pl.ds(items + g * ROWS, ROWS),
+            (x[1] - x[0]) * (m[0] * m[1]),
+            (x[5] - x[4]) * (m[4] * m[5]),
+        )
+        if g == 0:
+            for copy in row_copies[1:]:
+                copy.wait()
+        for k in range(first, first + group):
+            values = (
+                diff_v[k, 0:1, :],
+                diff_v[k, 1:2, :],
+                diff_v[k, rows - 2 : rows - 1, :],
+                diff_v[k, rows - 1 : rows, :],
+                north_v[0, k, 0:1, :],
+                north_v[1, k, 6:7, :],
+                north_v[1, k, 7:8, :],
+                north_v[2, k, 0:1, :],
+                north_v[3, k, 6:7, :],
+                north_v[3, k, 7:8, :],
+            )
+            for n, y in enumerate(values):
+                own_lat_coef[n, k : k + 1, :] = y
+            for n, top in enumerate((values[3], values[6], values[9])):
+                low = values[0] if n == 0 else jnp.zeros_like(top)
+                r = base + n * levels + k
+                send_rows(slice(r, r + 1), low, top)
+        for at in chunks:
+            acc = [gathered[n, at, :] if g else jnp.zeros((ROWS, LANES), F32) for n in range(10)]
+            for k in range(first, first + group):
+                j = (k - first) * (tracers + 3)
+                for t in range(tracers):
+                    n = k * tracers + t
+                    turned = turned_v[j + t, at, :]
+                    acc[0] = jnp.where(couple == n, turned, acc[0])
+                    acc[1] = jnp.where(couple == (n - 1) % 64, turned, acc[1])
+                    acc[2] = jnp.where(lane == 2 * n + 2, turned, acc[2])
+                    acc[3] = jnp.where(lane == (2 * n - 3) % LANES, turned, acc[3])
+                n = k * tracers
+                for i in range(3):
+                    turned = turned_v[j + tracers + i, at, :]
+                    acc[4 + 2 * i] = jnp.where(couple == n, turned, acc[4 + 2 * i])
+                    acc[5 + 2 * i] = jnp.where(couple == (n - 1) % 64, turned, acc[5 + 2 * i])
+            for n in range(10):
+                gathered[n, at, :] = acc[n]
+    r = base + 3 * levels
+    send_rows(slice(r, r + 1), row_bottoms[0].astype(F32), row_bottoms[5].astype(F32))
+    for q in range(r + 1, pay_a.shape[0]):
+        zero_row = jnp.zeros((1, cols), F32)
+        send_rows(slice(q, q + 1), zero_row, zero_row)
+
+    lane = iota((rows, LANES), 1)
+    couple = lane // 2
+    even = lane % 2 == 0
+    head = lane % (2 * tracers) == 0
+    level_of = couple // tracers
+    inside = couple < items
+
+    def spread(xs):
+        xs = [jnp.where(head, turn(x, by), 0.0) for x, by in xs]
+        for by in (2, 4):
+            turned = [turn(x, by) for x in xs]
+            xs = [x + y for x, y in zip(xs, turned)]
+        return xs
+
+    def column_mask(c):
+        col = bottom_v[:, c : c + 1] if c >= 0 else bottom_v[:, cols + c : cols + c + 1]
+        ok = (level_of < jnp.broadcast_to(col, (rows, LANES))) & inside
+        return jnp.where(ok, 1.0, 0.0)
+
+    first_two, last_two, second, third_last, *coefs = [gathered[n] for n in range(10)]
     cells = [
         first_two, turn(first_two, -1), turn(second, -2),
         turn(third_last, 3), turn(last_two, 2), turn(last_two, 1),
     ]
-    head = lane % (2 * tracers) == 0
-
-    def spread(x, by):
-        x = jnp.where(head, turn(x, by), 0.0)
-        x = x + turn(x, 2)
-        return x + turn(x, 4)
-
-    d_cols = [spread(coefs[0][i], by) for i, by in ((0, 0), (0, -1), (1, 2), (1, 1))]
-    v_cols, s_cols = (
-        [spread(pair[i], by) for i, by in ((0, 0), (1, 2), (1, 1))] for pair in coefs[1:]
+    m = [column_mask(c) for c in (0, 1, 2, -3, -2, -1)]
+    four = [(0, 0), (0, -1), (1, 2), (1, 1)]
+    own_coefs = spread(
+        [(coefs[i], by) for i, by in four]
+        + [(coefs[2 + i], by) for i, by in four if by != -1]
+        + [(coefs[4 + i], by) for i, by in four if by != -1]
     )
-    level_of = couple // tracers
-    inside = couple < items
-
-    def column_mask(c):
-        col = bottom_v[:, c : c + 1] if c >= 0 else bottom_v[:, cols + c : cols + c + 1]
-        ok = (level_of < jnp.broadcast_to(col, (rows, LANES))) & inside
-        return jnp.where(ok, 1.0, 0.0)
-
-    m = [column_mask(c) for c in (0, 1, 2, -3, -2, -1)]
     jump_01 = (cells[1] - cells[0]) * (m[0] * m[1])
     jump_12 = (cells[2] - cells[1]) * (m[1] * m[2])
     jump_e0 = (cells[4] - cells[3]) * (m[3] * m[4])
     jump_e1 = (cells[5] - cells[4]) * (m[4] * m[5])
-
-    def pair(low, high):
-        return jnp.where(even, low, turn(high, 1))
-
-    odd_lon = lax.rem(lax.axis_index(lon_name), 2) == 1
-    odd_lat = lax.rem(lax.axis_index(lat_name), 2) == 1
-    east = (pair(cells[5], jump_e1), pair(d_cols[3], v_cols[2]), pair(s_cols[2], m[5]))
-    west = (pair(cells[0], jump_01), d_cols[0], pair(zero, m[0]))
+    zero = jnp.zeros((rows, LANES), F32)
+    lows = (cells[5], own_coefs[3], own_coefs[9], cells[0], own_coefs[0], zero)
+    highs = [turn(x, 1) for x in (jump_e1, own_coefs[6], m[5], jump_01, m[0])]
+    highs.insert(4, zero)
+    pays = [jnp.where(even, low, high) for low, high in zip(lows, highs)]
     for n in range(3):
-        pay_c[n] = jnp.where(odd_lon, west[n], east[n])
-        pay_d[n] = jnp.where(odd_lon, east[n], west[n])
-    for n, x in enumerate(
-        [cells[0], cells[1], jump_12, cells[4], cells[5], jump_e0] + d_cols + v_cols + s_cols
-    ):
+        pay_c[n] = jnp.where(odd_lon, pays[3 + n], pays[n])
+        pay_d[n] = jnp.where(odd_lon, pays[n], pays[3 + n])
+    for n, x in enumerate([cells[0], cells[1], jump_12, cells[4], cells[5], jump_e0] + own_coefs):
         own_lon[n] = x
-
-    for b in range(items // ROWS):
-        at = pl.ds(b * ROWS, ROWS)
-        level = (sub + b * ROWS) // tracers
-        m = [
-            jnp.where(level < jnp.broadcast_to(x, (ROWS, cols)), 1.0, 0.0) for x in row_bottoms
-        ]
-        x = [y * z for y, z in zip(block[b], m)]
-        j01 = (x[1] - x[0]) * (m[0] * m[1])
-        j12 = (x[2] - x[1]) * (m[1] * m[2])
-        k0 = (x[4] - x[3]) * (m[3] * m[4])
-        k1 = (x[5] - x[4]) * (m[4] * m[5])
-        for n, y in enumerate((x[0], x[1], j12, x[4], x[5], k0)):
-            own_lat[n, at, :] = y
-        pay_a[at, :] = jnp.where(odd_lat, x[0], x[5])
-        pay_b[at, :] = jnp.where(odd_lat, x[5], x[0])
-        at = pl.ds(items + b * ROWS, ROWS)
-        pay_a[at, :] = jnp.where(odd_lat, j01, k1)
-        pay_b[at, :] = jnp.where(odd_lat, k1, j01)
-    base = 2 * items
-    for k in range(levels):
-        values = (
-            diff_v[k, 0:1, :],
-            diff_v[k, 1:2, :],
-            diff_v[k, rows - 2 : rows - 1, :],
-            diff_v[k, rows - 1 : rows, :],
-            north_v[0, k, 0:1, :],
-            north_v[1, k, 6:7, :],
-            north_v[1, k, 7:8, :],
-            north_v[2, k, 0:1, :],
-            north_v[3, k, 6:7, :],
-            north_v[3, k, 7:8, :],
-        )
-        for n, y in enumerate(values):
-            own_lat_coef[n, k : k + 1, :] = y
-        for n, top in enumerate((values[3], values[6], values[9])):
-            low = values[0] if n == 0 else jnp.zeros_like(top)
-            r = base + n * levels + k
-            pay_a[r : r + 1, :] = jnp.where(odd_lat, low, top)
-            pay_b[r : r + 1, :] = jnp.where(odd_lat, top, low)
-    r = base + 3 * levels
-    low, top = row_bottoms[0].astype(F32), row_bottoms[5].astype(F32)
-    pay_a[r : r + 1, :] = jnp.where(odd_lat, low, top)
-    pay_b[r : r + 1, :] = jnp.where(odd_lat, top, low)
-    for q in range(r + 1, pay_a.shape[0]):
-        pay_a[q : q + 1, :] = jnp.zeros_like(low)
-        pay_b[q : q + 1, :] = jnp.zeros_like(low)
 
 
 def pack(tracer, east_vel, north_vel, diff, east_slope, north_slope, bottom):
     tracers, levels, rows, cols = tracer.shape
     items = tracers * levels
     lat_rows = -(-(2 * items + 3 * levels + 1) // ROWS) * ROWS
-    shape = jax.ShapeDtypeStruct
-    vmem = pl.BlockSpec(memory_space=pltpu.VMEM)
+    hbm = pl.BlockSpec(memory_space=pltpu.HBM)
 
     def body(*refs):
         pack_kernel(levels, tracers, rows, cols, "lon", "lat", *refs)
 
+    shapes = [
+        (lat_rows, cols),
+        (lat_rows, cols),
+        (3, rows, LANES),
+        (3, rows, LANES),
+        (16, rows, LANES),
+        (6, items, cols),
+        (10, levels, cols),
+    ]
     return pl.pallas_call(
         body,
         name="pack_edges",
-        in_specs=[pl.BlockSpec(memory_space=pltpu.HBM)] * 7,
-        out_specs=[vmem] * 7,
-        out_shape=[
-            shape((lat_rows, cols), F32),
-            shape((lat_rows, cols), F32),
-            shape((3, rows, LANES), F32),
-            shape((3, rows, LANES), F32),
-            shape((16, rows, LANES), F32),
-            shape((6, items, cols), F32),
-            shape((10, levels, cols), F32),
-        ],
+        in_specs=[hbm] * 7,
+        out_specs=[pl.BlockSpec(memory_space=pltpu.VMEM)] * 12,
+        out_shape=[pltpu.VMEM(x, F32) for x in shapes]
+        + [pltpu.VMEM(x.shape, x.dtype) for x in (tracer, east_vel, diff, east_slope, bottom)],
         scratch_shapes=[
-            pltpu.VMEM((tracers, levels, rows, cols), F32),
-            pltpu.VMEM((levels, rows, cols), F32),
-            pltpu.VMEM((levels, rows, cols), F32),
-            pltpu.VMEM((levels, rows, cols), F32),
             pltpu.VMEM((4, levels, ROWS, cols), F32),
-            pltpu.VMEM((rows, cols), jnp.int32),
-            pltpu.SemaphoreType.DMA((levels // 3, 4)),
+            pltpu.VMEM((10, rows, LANES), F32),
+            pltpu.VMEM((ROWS // tracers * (tracers + 3), rows, LANES), F32),
+            pltpu.SemaphoreType.DMA((levels * tracers // ROWS, 4)),
             pltpu.SemaphoreType.DMA((5,)),
         ],
         compiler_params=pltpu.CompilerParams(vmem_limit_bytes=VMEM_LIMIT),
@@ -264,20 +285,12 @@
 
 
 def interior_kernel(levels, tracers, rows, cols, span, *refs):
-    sources = refs[:6]
-    bottom_hbm, explicit_hbm = refs[6], refs[-23]
+    tracer, east_vel, north_vel_hbm, diff, east_slope, north_slope_hbm, bottom, explicit = refs[:8]
+    sources = (north_vel_hbm, north_slope_hbm)
     (
-        tracer,
-        east_vel,
         north_vel,
-        diff,
-        east_slope,
         north_slope,
-        bottom,
-        explicit,
         sems,
-        bottom_sem,
-        out_sems,
         ring,
         ring_sum,
         step_here,
@@ -289,7 +302,7 @@
         north_part,
         open_at,
         coef,
-    ) = refs[-22:]
+    ) = refs[8:]
     first, stop = span()
     blocks = rows // ROWS
     halves = (slice(0, LANES), slice(LANES, 2 * LANES))
@@ -349,17 +362,8 @@
     units = [(t, b) for b in range(blocks) for t in range(tracers)]
 
     def fetch(n, level):
-        src, dst = sources[n], (tracer, east_vel, north_vel, diff, east_slope, north_slope)[n]
-        if n == 0:
-            src, dst = src.at[:, level], dst.at[:, level]
-        else:
-            src, dst = src.at[level], dst.at[level]
-        return pltpu.make_async_copy(src, dst, sems.at[n, level])
-
-    def store(level):
-        return pltpu.make_async_copy(
-            explicit.at[:, level], explicit_hbm.at[:, level], out_sems.at[level]
-        )
+        dst = (north_vel, north_slope)[n]
+        return pltpu.make_async_copy(sources[n].at[level], dst.at[level], sems.at[n, level])
 
     def each_level(low, high, body):
         def run(level, carry):
@@ -386,25 +390,13 @@
         for t, b in units:
             save(step_west, west_of(load(step_here, out, t, b)), out, t, b)
 
-    before_first = jnp.maximum(first - 1, 0)
-    past_last = jnp.minimum(stop + 1, levels)
-    started = first < stop
-
-    @pl.when(started)
+    @pl.when(first < stop)
     def _():
-        at_bottom = pltpu.make_async_copy(bottom_hbm, bottom, bottom_sem)
-        at_bottom.start()
-
         def begin(level):
-            fetch(0, level).start()
-
-            @pl.when((level >= first) & (level < stop))
-            def _():
-                for n in range(1, 6):
-                    fetch(n, level).start()
-
-        each_level(before_first, past_last, begin)
-        at_bottom.wait()
+            for n in range(2):
+                fetch(n, level).start()
+
+        each_level(first, stop, begin)
         depth = [load(bottom, b) for b in range(blocks)]
         ups, downs = [up(x) for x in depth], [down(x) for x in depth]
         east = [low2(x, east_of(x)) for x in depth]
@@ -436,11 +428,6 @@
                 5,
                 b,
             )
-        @pl.when(first > 0)
-        def _():
-            fetch(0, first - 1).wait()
-
-        fetch(0, first).wait()
         take_in(first - 1, lax.rem(first + 2, 3), lax.rem(first + 1, 2))
         take_in(first, lax.rem(first, 3), lax.rem(first, 2))
         take_steps(lax.rem(first, 2))
@@ -449,12 +436,8 @@
         now, later, before = lax.rem(level, 3), lax.rem(level + 1, 3), lax.rem(level + 2, 3)
         nth = lax.rem(level, 2)
         nth_next = 1 - nth
-        for n in range(1, 6):
+        for n in range(2):
             fetch(n, level).wait()
-
-        @pl.when(level + 1 < levels)
-        def _():
-            fetch(0, level + 1).wait()
 
         for t, b in units:
             bend = tuple(
@@ -564,13 +547,11 @@
             )
             save(explicit, total, t, level, b)
 
-        store(level).start()
 
     each_level(first, stop, one_level)
-    each_level(first, stop, lambda level: store(level).wait())
-
-
-def interior(tracer, east_vel, north_vel, diff, east_slope, north_slope, bottom, span, so_far=None):
+
+
+def interior(tracer, east_vel, north_vel, diff, east_slope, north_slope, bottom, span):
     tracers, levels, rows, cols = tracer.shape
 
     def body(*refs):
@@ -579,27 +560,18 @@
     plane = (tracers, rows, cols)
     field = pltpu.VMEM((levels, rows, cols), F32)
     args = (tracer, east_vel, north_vel, diff, east_slope, north_slope, bottom)
-    args = args if so_far is None else (*args, so_far)
     hbm = pl.BlockSpec(memory_space=pltpu.HBM)
+    vmem = pl.BlockSpec(memory_space=pltpu.VMEM)
     return pl.pallas_call(
         body,
         name="interior_faces",
-        in_specs=[hbm] * len(args),
-        out_specs=hbm,
-        out_shape=jax.ShapeDtypeStruct(tracer.shape, F32),
-        input_output_aliases={} if so_far is None else {7: 0},
+        in_specs=[vmem, vmem, hbm, vmem, vmem, hbm, vmem],
+        out_specs=vmem,
+        out_shape=pltpu.VMEM(tracer.shape, F32),
         scratch_shapes=[
-            pltpu.VMEM(tracer.shape, F32),
             field,
             field,
-            field,
-            field,
-            field,
-            pltpu.VMEM((rows, cols), jnp.int32),
-            pltpu.VMEM(tracer.shape, F32),
-            pltpu.SemaphoreType.DMA((6, levels)),
-            pltpu.SemaphoreType.DMA,
-            pltpu.SemaphoreType.DMA((levels,)),
+            pltpu.SemaphoreType.DMA((2, levels)),
             pltpu.VMEM((3, *plane), F32),
             pltpu.VMEM((3, *plane), F32),
             pltpu.VMEM((2, *plane), F32),
@@ -640,7 +612,7 @@
 
 def solve_kernel(levels, tracers, rows, cols, lon_name, lat_name, lat_count, *refs):
     (
-        explicit_hbm,
+        explicit,
         vertical_hbm,
         bottom,
         got_a,
@@ -675,13 +647,8 @@
 
     def fetch(b):
         at = rows_of(b)
-        return (
-            pltpu.make_async_copy(
-                explicit_hbm.at[:, :, at, :], field.at[:, :, at, :], in_sems.at[0, b]
-            ),
-            pltpu.make_async_copy(
-                vertical_hbm.at[:, at, :], vertical.at[:, at, :], in_sems.at[1, b]
-            ),
+        return pltpu.make_async_copy(
+            vertical_hbm.at[:, at, :], vertical.at[:, at, :], in_sems.at[b]
         )
 
     def store(b):
@@ -691,8 +658,7 @@
         )
 
     for b in range(blocks):
-        for copy in fetch(b):
-            copy.start()
+        fetch(b).start()
 
     def edges():
         odd_lon = lax.rem(lax.axis_index(lon_name), 2) == 1
@@ -840,25 +806,21 @@
 
     edges()
 
-    def one_block(step, carry):
+    def one_block(step, side):
         at = rows_of(step)
-        for copy in fetch(step):
-            copy.wait()
-        first_block = step == 0
-        row0 = jnp.where(first_block, 0, ROWS - 2)
-        pick = jnp.where(first_block, 0, 2)
-
-        @pl.when(first_block | (step == blocks - 1))
-        def _():
-            for t in range(tracers):
-                for k in range(levels):
-                    n = k * tracers + t
-                    for h in halves:
-                        low = jnp.broadcast_to(fix_lat[pick, n : n + 1, h], (ROWS, LANES))
-                        high = jnp.broadcast_to(fix_lat[pick + 1, n : n + 1, h], (ROWS, LANES))
-                        field[t, k, at, h] = field[t, k, at, h] + jnp.where(
-                            sub == row0, low, jnp.where(sub == row0 + 1, high, 0.0)
-                        )
+        fetch(step).wait()
+
+        def value_at(t, k, h):
+            if not side:
+                return explicit[t, k, at, h]
+            n = k * tracers + t
+            row0 = jnp.where(step == 0, 0, ROWS - 2)
+            pick = jnp.where(step == 0, 0, 2)
+            low = jnp.broadcast_to(fix_lat[pick, n : n + 1, h], (ROWS, LANES))
+            high = jnp.broadcast_to(fix_lat[pick + 1, n : n + 1, h], (ROWS, LANES))
+            return explicit[t, k, at, h] + jnp.where(
+                sub == row0, low, jnp.where(sub == row0 + 1, high, 0.0)
+            )
 
         depth = tuple(bottom[at, h] for h in halves)
         for i, h in enumerate(halves):
@@ -891,7 +853,7 @@
                 for k in range(levels):
                     turn = (begin - 2 * (k * tracers + t)) % LANES
                     patch = pltpu.roll(fixes[i], turn, axis=1) if turn else fixes[i]
-                    right = field[t, k, at, h] + jnp.where(near, patch, 0.0)
+                    right = value_at(t, k, h) + jnp.where(near, patch, 0.0)
                     right = jnp.where(depth[i] > k, right, 0.0)
                     if k:
                         right = right + pivots[1, k, :, h] * value
@@ -903,9 +865,15 @@
                     nxt = values[k] + pivots[2, k, :, h] * nxt
                     field[t, k, at, h] = nxt
         store(step).start()
-        return carry
-
-    lax.fori_loop(0, blocks, one_block, 0)
+
+    @pl.loop(0, 2)
+    def _(n):
+        one_block(n * (blocks - 1), True)
+
+    @pl.loop(1, blocks - 1)
+    def _(step):
+        one_block(step, False)
+
     for b in range(blocks):
         store(b).wait()
 
@@ -925,10 +893,9 @@
     return pl.pallas_call(
         body,
         name="edges_and_solve",
-        in_specs=[hbm, hbm] + [vmem] * 8,
+        in_specs=[vmem, hbm] + [vmem] * 8,
         out_specs=hbm,
         out_shape=jax.ShapeDtypeStruct(explicit.shape, F32),
-        input_output_aliases={0: 0},
         scratch_shapes=[
             pltpu.VMEM(explicit.shape, F32),
             pltpu.VMEM(vertical.shape, F32),
@@ -937,7 +904,7 @@
             pltpu.VMEM((lat_rows, cols), F32),
             pltpu.VMEM((lat_rows, cols), F32),
             pltpu.VMEM((3, levels, ROWS, cols), F32),
-            pltpu.SemaphoreType.DMA((2, blocks)),
+            pltpu.SemaphoreType.DMA((blocks,)),
             pltpu.SemaphoreType.DMA((blocks,)),
         ],
         compiler_params=pltpu.CompilerParams(vmem_limit_bytes=SOLVE_LIMIT),
@@ -960,8 +927,16 @@
 ):
     lon, lat = lax.axis_size("lon"), lax.axis_size("lat")
     levels = tracer.shape[1]
-    args = (tracer, east_velocity, north_velocity, diffusivity, east_slope, north_slope, bottom)
-    pay_a, pay_b, pay_c, pay_d, *own = pack(*args)
+    args = tuple(
+        pltpu.with_memory_space_constraint(x, pltpu.HBM)
+        for x in (
+            tracer, east_velocity, north_velocity, diffusivity, east_slope, north_slope, bottom
+        )
+    )
+    north = (args[2], args[5])
+    pay_a, pay_b, pay_c, pay_d, *own, held, held_vel, held_diff, held_slope, depth = pack(
+        *args
+    )
 
     def swap(pairs):
         return [p for a, b in pairs for p in ((a, b), (b, a))]
@@ -979,9 +954,12 @@
     got_c = lax.ppermute(pay_c, "lon", near_lon)
     got_b = lax.ppermute(pay_b, ("lon", "lat"), far_lat)
     got_d = lax.ppermute(pay_d, "lon", far_lon)
-    explicit = interior(*args, lambda: (0, levels))
+    explicit = interior(
+        held, held_vel, north[0], held_diff, held_slope, north[1], depth,
+        lambda: (0, levels),
+    )
     return solve(
-        explicit, vertical_diffusivity, bottom, (got_a, got_b, got_c, got_d), tuple(own)
+        explicit, vertical_diffusivity, depth, (got_a, got_b, got_c, got_d), tuple(own)
     )
 
 

time: 31.7 us -> 27.7 us (0.87)
  Pallas kernels: 20.8 us -> 17 us
    pallas_call x3, Pallas kernels: 20.8 us -> 17 us  [the longest x1 8.81 us: interior(): pl.pallas_call(body, name='interior_faces', in_specs=[vmem, vmem, hbm, vm...]
  transfers between devices with their start and end apart: 4 -> 4, of which waited for: 0 -> 0; matrix products, arithmetic and copies ran while one was open for 0% -> 0% of each run, Pallas kernels for 33% -> 32%
where the time goes in v2:
time: 27.7 us; the launch traced here: 27.6 us
  Pallas kernels  17 us (61%)
  starting transfers between devices  10.5 us (38%)
    pallas_call x1, Pallas kernels, interior(): pl.pallas_call(body, name='interior_faces', in_specs=[vmem, vmem, hbm, vm...  8.81 us
    ppermute x1, starting transfers between devices, local(): got_d = lax.ppermute(pay_d, 'lon', far_lon)  5.29 us
    pallas_call x1, Pallas kernels, pack(): pl.pallas_call(body, name='pack_edges', in_specs=[hbm] * 7, out_specs=[pl...  4.56 us
    pallas_call x1, Pallas kernels, solve(): pl.pallas_call(body, name='edges_and_solve', in_specs=[vmem, hbm] + [vmem...  3.63 us
    ppermute x1, starting transfers between devices, local(): got_b = lax.ppermute(pay_b, ('lon', 'lat'), far_lat)  3.06 us
    ppermute x1, starting transfers between devices, local(): got_c = lax.ppermute(pay_c, 'lon', near_lon)  2.1 us
  transfers between devices with their start and end apart: 4, of which 0 were waited for; matrix products, arithmetic and copies ran while one was open for 0% of the time, Pallas kernels for 32%

profile of v2, /device:TPU:4, one launch (start us, length us, event | category | flops | bytes accessed | tf_op | source)
XLA Modules:
  0.0 27.6 jit_solution(8888624351339527224)
XLA Ops:
  0.0 4.6 %pack_edges.1 = (f32[136,256]{1,0:T(8,128)S(1)}, f32[136,256]{1,0:T(8,128)S(1)}, f32[3,64,128]{2,1,0:T(8,128)S(1)}, f32[3,64,128]{2,1,0:T(8,128)S(1)}, f32[16,64...) custom-call(f32[4,12,64,256]{3,2,1,0:T(8,128)} %refs_0_.1, ...), custom_call_target="tpu_custom_call" | custom-call | flops 1000000 | bytes 7000000 | tf_op jit(solution)/shard_map/pack_edges/pallas_call | solution.py:268
  4.6 0.1 collective-permute-start
  4.7 3.1 %collective-permute-start.1 = (f32[136,256]{1,0:T(8,128)S(1)}, f32[136,256]{1,0:T(8,128)S(1)}, u32[]{:S(2)}, u32[]{:S(2)}) collective-permute-start(f32[136,256]{1,0:T(8,128)S(1)} %get-tuple-element.23), channel_id=1, source_target_pairs={{1,2},{2,1},{3,4},{4,3},{5,6},{6,5},{7,8},{8,7},{9,10},{10,9},{11,... | collective-permute-start | bytes 417800 | tf_op jit(solution)/shard_map/ppermute | solution.py:955
  7.7 2.1 %collective-permute-start.2 = (f32[3,64,128]{2,1,0:T(8,128)S(1)}, f32[3,64,128]{2,1,0:T(8,128)S(1)}, u32[]{:S(2)}, u32[]{:S(2)}) collective-permute-start(f32[3,64,128]{2,1,0:T(8,128)S(1)} %get-tuple-element.24), channel_id=1, source_target_pairs={{0,16},{16,0},{32,48},{48,32},{64,80},{80,64},{96,112},{112,96},{1... | collective-permute-start | bytes 294920 | tf_op jit(solution)/shard_map/ppermute | solution.py:954
  9.8 5.3 %collective-permute-start.3 = (f32[3,64,128]{2,1,0:T(8,128)S(1)}, f32[3,64,128]{2,1,0:T(8,128)S(1)}, u32[]{:S(2)}, u32[]{:S(2)}) collective-permute-start(f32[3,64,128]{2,1,0:T(8,128)S(1)} %get-tuple-element.25), channel_id=1, source_target_pairs={{16,32},{32,16},{48,64},{64,48},{80,96},{96,80},{112,128},{128,112... | collective-permute-start | bytes 294920 | tf_op jit(solution)/shard_map/ppermute | solution.py:956
  15.1 0.0 copy-start
  15.1 8.8 %interior_faces.1.refs_0_ = f32[4,12,64,256]{3,2,1,0:T(8,128)S(1)} custom-call(f32[4,12,64,256]{3,2,1,0:T(8,128)S(1)} %get-tuple-element.17.refs_0_, f32[12,64,256]{2,1,0:T(8,128)S(1)} %get-tuple-element.18.refs_1_, f32[12,64,256]{2,1,0:T(8,128)} %refs_2_.3, f32[12,64,256]{2,1,0:T(8,128)S(1)} %get-tuple-element.19.refs_3_, ...), custom_call_target="tpu_custom_call" | custom-call | flops 47185920 | bytes 12000000 | tf_op jit(solution)/shard_map/interior_faces/pallas_call | solution.py:565
  23.9 0.0 collective-permute-done.2.refs_5_
  24.0 0.0 collective-permute-done.3.refs_6_
  24.0 0.0 collective-permute-done.refs_3_
  24.0 0.0 collective-permute-done.1.refs_4_
  24.0 0.0 copy-done
  24.0 3.6 %edges_and_solve.1 = f32[4,12,64,256]{3,2,1,0:T(8,128)} custom-call(f32[4,12,64,256]{3,2,1,0:T(8,128)S(1)} %interior_faces.1.refs_0_, f32[11,64,256]{2,1,0:T(8,128)S(1)} %copy-done, s32[64,256]{1,0:T(8,128)S(1)} %get-tuple-element.21.refs_6_.refs_2_, f32[136,256]{1,0:T(8,128)S(1)} %collective-permute-done.refs_3_, ...), custom_call_target="tpu_custom_call" | custom-call | flops 15728640 | bytes 8000000 | tf_op jit(solution)/shard_map/edges_and_solve/pallas_call | solution.py:893
Async XLA Ops:
  4.6 19.4 %collective-permute-start = (f32[136,256]{1,0:T(8,128)S(1)}, f32[136,256]{1,0:T(8,128)S(1)}, u32[]{:S(2)}, u32[]{:S(2)}) collective-permute-start(f32[136,256]{1,0:T(8,128)S(1)} %get-tuple-element.22), channel_id=1, source_target_pairs={{0,1},{1,0},{2,3},{3,2},{4,5},{5,4},{6,7},{7,6},{8,9},{9,8},{10,11... | collective-permute-start | bytes 417800 | tf_op jit(solution)/shard_map/ppermute | solution.py:953
  4.7 19.3 %collective-permute-start.1 = (f32[136,256]{1,0:T(8,128)S(1)}, f32[136,256]{1,0:T(8,128)S(1)}, u32[]{:S(2)}, u32[]{:S(2)}) collective-permute-start(f32[136,256]{1,0:T(8,128)S(1)} %get-tuple-element.23), channel_id=1, source_target_pairs={{1,2},{2,1},{3,4},{4,3},{5,6},{6,5},{7,8},{8,7},{9,10},{10,9},{11,... | collective-permute-start | bytes 417800 | tf_op jit(solution)/shard_map/ppermute | solution.py:955
  7.7 16.2 %collective-permute-start.2 = (f32[3,64,128]{2,1,0:T(8,128)S(1)}, f32[3,64,128]{2,1,0:T(8,128)S(1)}, u32[]{:S(2)}, u32[]{:S(2)}) collective-permute-start(f32[3,64,128]{2,1,0:T(8,128)S(1)} %get-tuple-element.24), channel_id=1, source_target_pairs={{0,16},{16,0},{32,48},{48,32},{64,80},{80,64},{96,112},{112,96},{1... | collective-permute-start | bytes 294920 | tf_op jit(solution)/shard_map/ppermute | solution.py:954
  9.8 14.1 %collective-permute-start.3 = (f32[3,64,128]{2,1,0:T(8,128)S(1)}, f32[3,64,128]{2,1,0:T(8,128)S(1)}, u32[]{:S(2)}, u32[]{:S(2)}) collective-permute-start(f32[3,64,128]{2,1,0:T(8,128)S(1)} %get-tuple-element.25), channel_id=1, source_target_pairs={{16,32},{32,16},{48,64},{64,48},{80,96},{96,80},{112,128},{128,112... | collective-permute-start | bytes 294920 | tf_op jit(solution)/shard_map/ppermute | solution.py:956
  15.1 8.9 %copy-start = (f32[11,64,256]{2,1,0:T(8,128)S(1)}, f32[11,64,256]{2,1,0:T(8,128)}, u32[]{:S(2)}) copy-start(f32[11,64,256]{2,1,0:T(8,128)} %refs_1_.3) | copy-start | bytes 2162692

commit v3 on v2

--- a/solution.py
+++ b/solution.py
@@ -8,7 +8,7 @@
 F32 = jnp.float32
 LANES = 128
 ROWS = 8
-VMEM_LIMIT = 40 << 20
+VMEM_LIMIT = 36 << 20
 SOLVE_LIMIT = 32 << 20
 
 
@@ -42,12 +42,22 @@
         diff_v,
         east_slope_v,
         bottom_v,
+        north_vel_v,
+        north_slope_v,
+        open_at,
+        explicit,
+        ring,
+        ring_sum,
+        step_here,
+        step_west,
         north_v,
         gathered,
         turned_v,
         sems,
         row_sems,
-    ) = refs[7:]
+        north_sems,
+    ) = refs[7:33]
+    scratch = refs[33:]
     tracer_hbm, east_vel_hbm, north_vel_hbm, diff_hbm, east_slope_hbm, north_slope_hbm = sources[:6]
     items = levels * tracers
     group = ROWS // tracers
@@ -106,9 +116,16 @@
 
     row_copies[0].wait()
     row_bottoms = [bottom_v[r : r + 1, :] for r in row_at]
+    north_copies = [
+        pltpu.make_async_copy(north_vel_hbm, north_vel_v, north_sems.at[0]),
+        pltpu.make_async_copy(north_slope_hbm, north_slope_v, north_sems.at[1]),
+    ]
     for g in range(groups):
         for copy in copies[g]:
             copy.wait()
+        if g == groups - 1:
+            for copy in north_copies:
+                copy.start()
         for k in range(g * group, (g + 1) * group):
             j = (k - g * group) * (tracers + 3)
             for at in chunks:
@@ -246,6 +263,16 @@
     for n, x in enumerate([cells[0], cells[1], jump_12, cells[4], cells[5], jump_e0] + own_coefs):
         own_lon[n] = x
 
+    for copy in north_copies:
+        copy.wait()
+    interior_stage(
+        levels, tracers, rows, 0, levels_ahead(levels), True,
+        (
+            tracer_v, east_vel_v, north_vel_v, diff_v, east_slope_v, north_slope_v, bottom_v,
+            open_at, explicit, ring, ring_sum, step_here, step_west, *scratch,
+        ),
+    )
+
 
 def pack(tracer, east_vel, north_vel, diff, east_slope, north_slope, bottom):
     tracers, levels, rows, cols = tracer.shape
@@ -269,28 +296,39 @@
         body,
         name="pack_edges",
         in_specs=[hbm] * 7,
-        out_specs=[pl.BlockSpec(memory_space=pltpu.VMEM)] * 12,
+        out_specs=[pl.BlockSpec(memory_space=pltpu.VMEM)] * 20,
         out_shape=[pltpu.VMEM(x, F32) for x in shapes]
-        + [pltpu.VMEM(x.shape, x.dtype) for x in (tracer, east_vel, diff, east_slope, bottom)],
+        + [
+            pltpu.VMEM(x.shape, x.dtype)
+            for x in (tracer, east_vel, diff, east_slope, bottom, north_vel, north_slope)
+        ]
+        + [pltpu.VMEM((6, rows, cols), jnp.int32), pltpu.VMEM(tracer.shape, F32)]
+        + [pltpu.VMEM((n, tracers, rows, cols), F32) for n in (3, 3, 2, 2)],
         scratch_shapes=[
             pltpu.VMEM((4, levels, ROWS, cols), F32),
             pltpu.VMEM((10, rows, LANES), F32),
             pltpu.VMEM((ROWS // tracers * (tracers + 3), rows, LANES), F32),
             pltpu.SemaphoreType.DMA((levels * tracers // ROWS, 4)),
             pltpu.SemaphoreType.DMA((5,)),
+            pltpu.SemaphoreType.DMA((2,)),
+            *stage_scratch(tracers, rows, cols),
         ],
         compiler_params=pltpu.CompilerParams(vmem_limit_bytes=VMEM_LIMIT),
         cost_estimate=pl.CostEstimate(flops=10**6, bytes_accessed=7 * 10**6, transcendentals=0),
     )(tracer, east_vel, north_vel, diff, east_slope, north_slope, bottom)
 
 
-def interior_kernel(levels, tracers, rows, cols, span, *refs):
-    tracer, east_vel, north_vel_hbm, diff, east_slope, north_slope_hbm, bottom, explicit = refs[:8]
-    sources = (north_vel_hbm, north_slope_hbm)
+def interior_stage(levels, tracers, rows, first, stop, fresh, refs):
     (
+        tracer,
+        east_vel,
         north_vel,
+        diff,
+        east_slope,
         north_slope,
-        sems,
+        bottom,
+        open_at,
+        explicit,
         ring,
         ring_sum,
         step_here,
@@ -300,10 +338,9 @@
         flux_west,
         partial,
         north_part,
-        open_at,
         coef,
-    ) = refs[8:]
-    first, stop = span()
+    ) = refs
+    cols = 2 * LANES
     blocks = rows // ROWS
     halves = (slice(0, LANES), slice(LANES, 2 * LANES))
     lane = iota((ROWS, LANES), 1)
@@ -360,10 +397,6 @@
         return tuple(jnp.minimum(p, q) for p, q in zip(x, y))
 
     units = [(t, b) for b in range(blocks) for t in range(tracers)]
-
-    def fetch(n, level):
-        dst = (north_vel, north_slope)[n]
-        return pltpu.make_async_copy(sources[n].at[level], dst.at[level], sems.at[n, level])
 
     def each_level(low, high, body):
         def run(level, carry):
@@ -390,13 +423,7 @@
         for t, b in units:
             save(step_west, west_of(load(step_here, out, t, b)), out, t, b)
 
-    @pl.when(first < stop)
-    def _():
-        def begin(level):
-            for n in range(2):
-                fetch(n, level).start()
-
-        each_level(first, stop, begin)
+    if fresh:
         depth = [load(bottom, b) for b in range(blocks)]
         ups, downs = [up(x) for x in depth], [down(x) for x in depth]
         east = [low2(x, east_of(x)) for x in depth]
@@ -428,17 +455,14 @@
                 5,
                 b,
             )
-        take_in(first - 1, lax.rem(first + 2, 3), lax.rem(first + 1, 2))
-        take_in(first, lax.rem(first, 3), lax.rem(first, 2))
-        take_steps(lax.rem(first, 2))
+        take_in(-1, 2, 1)
+        take_in(0, 0, 0)
+        take_steps(0)
 
     def one_level(level):
         now, later, before = lax.rem(level, 3), lax.rem(level + 1, 3), lax.rem(level + 2, 3)
         nth = lax.rem(level, 2)
         nth_next = 1 - nth
-        for n in range(2):
-            fetch(n, level).wait()
-
         for t, b in units:
             bend = tuple(
                 minmod(x, y)
@@ -551,44 +575,40 @@
     each_level(first, stop, one_level)
 
 
-def interior(tracer, east_vel, north_vel, diff, east_slope, north_slope, bottom, span):
-    tracers, levels, rows, cols = tracer.shape
+def stage_scratch(tracers, rows, cols):
+    return [pltpu.VMEM((tracers, rows, cols), F32)] * 5 + [pltpu.VMEM((8, rows, cols), F32)]
+
+
+def levels_ahead(levels):
+    lead = lax.axis_size("lon") // 4
+    early = jnp.maximum(lead - lax.axis_index("lon") // 2, 0)
+    return (levels * early) // (2 * lead)
+
+
+def interior_rest(held, state):
+    tracers, levels, rows, cols = held[0].shape
 
     def body(*refs):
-        interior_kernel(levels, tracers, rows, cols, span, *refs)
-
-    plane = (tracers, rows, cols)
-    field = pltpu.VMEM((levels, rows, cols), F32)
-    args = (tracer, east_vel, north_vel, diff, east_slope, north_slope, bottom)
-    hbm = pl.BlockSpec(memory_space=pltpu.HBM)
+        given, changed, scratch = refs[:8], refs[13:18], refs[18:]
+        interior_stage(
+            levels, tracers, rows, levels_ahead(levels), levels, False,
+            (*given, *changed, *scratch),
+        )
+
     vmem = pl.BlockSpec(memory_space=pltpu.VMEM)
     return pl.pallas_call(
         body,
         name="interior_faces",
-        in_specs=[vmem, vmem, hbm, vmem, vmem, hbm, vmem],
-        out_specs=vmem,
-        out_shape=pltpu.VMEM(tracer.shape, F32),
-        scratch_shapes=[
-            field,
-            field,
-            pltpu.SemaphoreType.DMA((2, levels)),
-            pltpu.VMEM((3, *plane), F32),
-            pltpu.VMEM((3, *plane), F32),
-            pltpu.VMEM((2, *plane), F32),
-            pltpu.VMEM((2, *plane), F32),
-            pltpu.VMEM(plane, F32),
-            pltpu.VMEM(plane, F32),
-            pltpu.VMEM(plane, F32),
-            pltpu.VMEM(plane, F32),
-            pltpu.VMEM(plane, F32),
-            pltpu.VMEM((6, rows, cols), jnp.int32),
-            pltpu.VMEM((8, rows, cols), F32),
-        ],
+        in_specs=[vmem] * 13,
+        out_specs=[vmem] * 5,
+        out_shape=[pltpu.VMEM(x.shape, F32) for x in state],
+        input_output_aliases={8 + n: n for n in range(5)},
+        scratch_shapes=stage_scratch(tracers, rows, cols),
         compiler_params=pltpu.CompilerParams(vmem_limit_bytes=VMEM_LIMIT),
         cost_estimate=pl.CostEstimate(
-            flops=60 * tracer.size, bytes_accessed=12 * 10**6, transcendentals=0
+            flops=60 * held[0].size, bytes_accessed=12 * 10**6, transcendentals=0
         ),
-    )(*args)
+    )(*held, *state)[0]
 
 
 def edge_faces(m1, m2, m3, j0, j3, open1, open2, d1, d2, d3, v0, v1, s0, s1, tilt):
@@ -926,17 +946,15 @@
     bottom,
 ):
     lon, lat = lax.axis_size("lon"), lax.axis_size("lat")
-    levels = tracer.shape[1]
     args = tuple(
         pltpu.with_memory_space_constraint(x, pltpu.HBM)
         for x in (
             tracer, east_velocity, north_velocity, diffusivity, east_slope, north_slope, bottom
         )
     )
-    north = (args[2], args[5])
-    pay_a, pay_b, pay_c, pay_d, *own, held, held_vel, held_diff, held_slope, depth = pack(
-        *args
-    )
+    pay_a, pay_b, pay_c, pay_d, *kept = pack(*args)
+    own, (held, held_vel, held_diff, held_slope, depth) = kept[:3], kept[3:8]
+    north_vel, north_slope, open_at, *state = kept[8:]
 
     def swap(pairs):
         return [p for a, b in pairs for p in ((a, b), (b, a))]
@@ -954,9 +972,8 @@
     got_c = lax.ppermute(pay_c, "lon", near_lon)
     got_b = lax.ppermute(pay_b, ("lon", "lat"), far_lat)
     got_d = lax.ppermute(pay_d, "lon", far_lon)
-    explicit = interior(
-        held, held_vel, north[0], held_diff, held_slope, north[1], depth,
-        lambda: (0, levels),
+    explicit = interior_rest(
+        (held, held_vel, north_vel, held_diff, held_slope, north_slope, depth, open_at), state
     )
     return solve(
         explicit, vertical_diffusivity, depth, (got_a, got_b, got_c, got_d), tuple(own)

time: 27.7 us -> 25.3 us (0.913)
  starting transfers between devices: 10.5 us -> 6.83 us
  waiting for transfers between devices: 0.01 us -> 1.49 us
    pallas_call x1, Pallas kernels: 8.81 us -> 3.64 us  [interior_rest(): pl.pallas_call(body, name='interior_faces', in_specs=[vmem] * 13, out_spe...]
    pallas_call x1, Pallas kernels: 4.56 us -> 9.55 us  [pack(): pl.pallas_call(body, name='pack_edges', in_specs=[hbm] * 7, out_specs=[pl...]
    ppermute x1, starting transfers between devices: 5.29 us -> 1.58 us  [local(): got_d = lax.ppermute(pay_d, 'lon', far_lon)]
    ppermute x1, waiting for transfers between devices: 0.01 us -> 1.48 us  [local(): got_d = lax.ppermute(pay_d, 'lon', far_lon)]
  transfers between devices with their start and end apart: 4 -> 4, of which waited for: 0 -> 1; matrix products, arithmetic and copies ran while one was open for 0% -> 0% of each run, Pallas kernels for 32% -> 14%
where the time goes in v3:
time: 25.3 us; the launch traced here: 25.2 us
  Pallas kernels  16.8 us (66%)
  starting transfers between devices  6.83 us (27%)
  waiting for transfers between devices  1.49 us (6%)
    pallas_call x1, Pallas kernels, pack(): pl.pallas_call(body, name='pack_edges', in_specs=[hbm] * 7, out_specs=[pl...  9.55 us
    pallas_call x1, Pallas kernels, interior_rest(): pl.pallas_call(body, name='interior_faces', in_specs=[vmem] * 13, out_spe...  3.64 us
    pallas_call x1, Pallas kernels, solve(): pl.pallas_call(body, name='edges_and_solve', in_specs=[vmem, hbm] + [vmem...  3.63 us
    ppermute x1, starting transfers between devices, local(): got_b = lax.ppermute(pay_b, ('lon', 'lat'), far_lat)  3.06 us
    ppermute x1, starting transfers between devices, local(): got_c = lax.ppermute(pay_c, 'lon', near_lon)  2.1 us
    ppermute x1, starting transfers between devices, local(): got_d = lax.ppermute(pay_d, 'lon', far_lon)  1.58 us
    ppermute x1, waiting for transfers between devices, local(): got_d = lax.ppermute(pay_d, 'lon', far_lon)  1.48 us
  transfers between devices with their start and end apart: 4, of which 1 were waited for; matrix products, arithmetic and copies ran while one was open for 0% of the time, Pallas kernels for 14%

profile of v3, /device:TPU:4, one launch (start us, length us, event | category | flops | bytes accessed | tf_op | source)
XLA Modules:
  0.0 25.2 jit_solution(4087846959949579241)
XLA Ops:
  0.0 9.6 %pack_edges.1 = (f32[136,256]{1,0:T(8,128)S(1)}, f32[136,256]{1,0:T(8,128)S(1)}, f32[3,64,128]{2,1,0:T(8,128)S(1)}, f32[3,64,128]{2,1,0:T(8,128)S(1)}, f32[16,64...) custom-call(f32[4,12,64,256]{3,2,1,0:T(8,128)} %refs_0_.1, ...), custom_call_target="tpu_custom_call" | custom-call | flops 1000000 | bytes 7000000 | tf_op jit(solution)/shard_map/pack_edges/pallas_call | solution.py:295
  9.6 0.1 collective-permute-start
  9.7 3.1 %collective-permute-start.1 = (f32[136,256]{1,0:T(8,128)S(1)}, f32[136,256]{1,0:T(8,128)S(1)}, u32[]{:S(2)}, u32[]{:S(2)}) collective-permute-start(f32[136,256]{1,0:T(8,128)S(1)} %get-tuple-element.41), channel_id=1, source_target_pairs={{1,2},{2,1},{3,4},{4,3},{5,6},{6,5},{7,8},{8,7},{9,10},{10,9},{11,... | collective-permute-start | bytes 417800 | tf_op jit(solution)/shard_map/ppermute | solution.py:973
  12.7 2.1 %collective-permute-start.2 = (f32[3,64,128]{2,1,0:T(8,128)S(1)}, f32[3,64,128]{2,1,0:T(8,128)S(1)}, u32[]{:S(2)}, u32[]{:S(2)}) collective-permute-start(f32[3,64,128]{2,1,0:T(8,128)S(1)} %get-tuple-element.42), channel_id=1, source_target_pairs={{0,16},{16,0},{32,48},{48,32},{64,80},{80,64},{96,112},{112,96},{1... | collective-permute-start | bytes 294920 | tf_op jit(solution)/shard_map/ppermute | solution.py:972
  14.8 1.6 %collective-permute-start.3 = (f32[3,64,128]{2,1,0:T(8,128)S(1)}, f32[3,64,128]{2,1,0:T(8,128)S(1)}, u32[]{:S(2)}, u32[]{:S(2)}) collective-permute-start(f32[3,64,128]{2,1,0:T(8,128)S(1)} %get-tuple-element.43), channel_id=1, source_target_pairs={{16,32},{32,16},{48,64},{64,48},{80,96},{96,80},{112,128},{128,112... | collective-permute-start | bytes 294920 | tf_op jit(solution)/shard_map/ppermute | solution.py:974
  16.4 0.0 copy-start
  16.4 3.6 %interior_faces.1 = (f32[4,12,64,256]{3,2,1,0:T(8,128)S(1)}, f32[3,4,64,256]{3,2,1,0:T(8,128)S(1)}, f32[3,4,64,256]{3,2,1,0:T(8,128)S(1)}, f32[2,4,64,256]{3,2,1,0:T(8,128)S(1)}, f32[2,4,64,256]{3,2,1,0:T(8,128)S(1)}) custom-call(f32[4,12,64,256]{3,2,1,0:T(8,128)S(1)} %get-tuple-elemen, ...), custom_call_target="tpu_custom_call", output_to_operand_aliasing={{0}: (8, {}), {1}: (9, {}), {2}: (10, {}), {3}: (11, {}), {... | custom-call | flops 47185920 | bytes 12000000 | tf_op jit(solution)/shard_map/interior_faces/pallas_call | solution.py:599
  20.1 0.0 collective-permute-done.2.refs_5_
  20.1 1.5 %collective-permute-done.3.refs_6_ = f32[3,64,128]{2,1,0:T(8,128)S(1)} collective-permute-done((f32[3,64,128]{2,1,0:T(8,128)S(1)}, f32[3,64,128]{2,1,0:T(8,128)S(1)}, u32[]{:S(2)}, u32[]{:S(2)}) %collective-permute-start.3) | collective-permute-done | bytes 98336 | tf_op jit(solution)/shard_map/ppermute | solution.py:974
  21.5 0.0 collective-permute-done.refs_3_
  21.6 0.0 collective-permute-done.1.refs_4_
  21.6 0.0 copy-done
  21.6 3.6 %edges_and_solve.1 = f32[4,12,64,256]{3,2,1,0:T(8,128)} custom-call(f32[4,12,64,256]{3,2,1,0:T(8,128)S(1)} %get-tuple-element.39.refs_0_, f32[11,64,256]{2,1,0:T(8,128)S(1)} %copy-done, s32[64,256]{1,0:T(8,128)S(1)} %get-tuple-element.32.refs_6_.refs_2_, f32[136,256]{1,0:T(8,128)S(1)} %collective-permute-done.refs_3_, ...), custom_call_target="tpu_custom_call" | custom-call | flops 15728640 | bytes 8000000 | tf_op jit(solution)/shard_map/edges_and_solve/pallas_call | solution.py:913
Async XLA Ops:
  9.6 12.0 %collective-permute-start = (f32[136,256]{1,0:T(8,128)S(1)}, f32[136,256]{1,0:T(8,128)S(1)}, u32[]{:S(2)}, u32[]{:S(2)}) collective-permute-start(f32[136,256]{1,0:T(8,128)S(1)} %get-tuple-element.40), channel_id=1, source_target_pairs={{0,1},{1,0},{2,3},{3,2},{4,5},{5,4},{6,7},{7,6},{8,9},{9,8},{10,11... | collective-permute-start | bytes 417800 | tf_op jit(solution)/shard_map/ppermute | solution.py:971
  9.7 11.9 %collective-permute-start.1 = (f32[136,256]{1,0:T(8,128)S(1)}, f32[136,256]{1,0:T(8,128)S(1)}, u32[]{:S(2)}, u32[]{:S(2)}) collective-permute-start(f32[136,256]{1,0:T(8,128)S(1)} %get-tuple-element.41), channel_id=1, source_target_pairs={{1,2},{2,1},{3,4},{4,3},{5,6},{6,5},{7,8},{8,7},{9,10},{10,9},{11,... | collective-permute-start | bytes 417800 | tf_op jit(solution)/shard_map/ppermute | solution.py:973
  12.7 7.3 %collective-permute-start.2 = (f32[3,64,128]{2,1,0:T(8,128)S(1)}, f32[3,64,128]{2,1,0:T(8,128)S(1)}, u32[]{:S(2)}, u32[]{:S(2)}) collective-permute-start(f32[3,64,128]{2,1,0:T(8,128)S(1)} %get-tuple-element.42), channel_id=1, source_target_pairs={{0,16},{16,0},{32,48},{48,32},{64,80},{80,64},{96,112},{112,96},{1... | collective-permute-start | bytes 294920 | tf_op jit(solution)/shard_map/ppermute | solution.py:972
  14.8 6.7 %collective-permute-start.3 = (f32[3,64,128]{2,1,0:T(8,128)S(1)}, f32[3,64,128]{2,1,0:T(8,128)S(1)}, u32[]{:S(2)}, u32[]{:S(2)}) collective-permute-start(f32[3,64,128]{2,1,0:T(8,128)S(1)} %get-tuple-element.43), channel_id=1, source_target_pairs={{16,32},{32,16},{48,64},{64,48},{80,96},{96,80},{112,128},{128,112... | collective-permute-start | bytes 294920 | tf_op jit(solution)/shard_map/ppermute | solution.py:974
  16.4 5.2 %copy-start = (f32[11,64,256]{2,1,0:T(8,128)S(1)}, f32[11,64,256]{2,1,0:T(8,128)}, u32[]{:S(2)}) copy-start(f32[11,64,256]{2,1,0:T(8,128)} %refs_1_.3) | copy-start | bytes 2162692
